TPU v7x, 256 devices: a whole 4x4x8 slice. The times are simulated.
256 devices in a mesh: tm: 16 (over z, core), lon: 8 (over y, x_lo), ens: 2 (over x_hi).
Axes of the slice: x: 4 (x_hi: 2, x_lo: 2; x = x_hi * 2 + x_lo), y: 4, z: 8, core: 2. Of those that a mesh axis runs over, the one named last changes fastest.
Arguments:
- anomalies: bfloat16 [8192, 1024], P('lon', 'ens'), may hold values from -6 to 6
- localization: bfloat16 [64, 3, 128, 128], P('lon'), may hold values from -0.3125 to 0.3125
- innovations: float32 [16, 4096], P('tm', 'lon'), may hold values from -6 to 6
- obs_cell: int32 [16, 4096], P('tm', 'lon'), may hold values from 0 to 1023
- tangent_blocks: float32 [16, 8, 128, 128], P('tm'), may hold values from -1 to 2
- tangent_order: int32 [16, 8], P('tm'), may hold values from 0 to 7, each once within a row
Outputs:
- forward_states: float32 [16, 1024, 1024], P('tm', ('ens', 'lon'))
- adjoint_states: float32 [16, 1024, 1024], P('tm', ('ens', 'lon'))
Inputs may be any that keep to these rules, and one draw needn't show every extreme that they name: Observation j of a step lies in sector j // 512, at that sector's cell obs_cell. `tangent_order`: each step's row names every block index once.
All inputs are finite; a program needn't handle non-finite values.
Results may differ from a plain program's by a relative error of at most 0.015.
Values may be sent and summed in bfloat16 or wider, within the bound.
No kernel may reach another device: no remote copies, remote signals or barrier semaphores. Data moves between devices by JAX's collectives and lax.ppermute only.
A program may use at most 64 MiB of HBM per device.

v0:
```python
import functools

import jax
import jax.numpy as jnp
from jax import lax
from jax.experimental import pallas as pl
from jax.experimental.pallas import tpu as pltpu
from jax.sharding import Mesh
from jax.sharding import PartitionSpec as P

BLK = 128
NB = 8
COLS = NB * BLK
bf16 = jnp.bfloat16
f32 = jnp.float32

VM = pl.BlockSpec(memory_space=pltpu.VMEM)
SM = pl.BlockSpec(memory_space=pltpu.SMEM)
ANY = pl.BlockSpec(memory_space=pl.ANY)

MSG = COLS + 16
HALF = COLS // 2 + 16
MIB = 1024 * 1024


def call(kernel, outs, ins, scratch=(), flops=0, data=0, grant=16, specs=None):
    return pl.pallas_call(
        kernel,
        out_shape=outs,
        in_specs=ins,
        out_specs=specs or [VM] * len(outs),
        scratch_shapes=list(scratch),
        compiler_params=pltpu.CompilerParams(vmem_limit_bytes=grant * MIB),
        cost_estimate=pl.CostEstimate(flops=flops, bytes_accessed=data, transcendentals=0),
    )


def split(x):
    hi = x.astype(bf16)
    lo = (x - hi.astype(f32)).astype(bf16)
    return jnp.concatenate([hi, lo], axis=0)


def cols_at(i):
    return pl.ds(pl.multiple_of(i * BLK, BLK), BLK)


def entry_kernel(innov, cell, anom, tang, order, out, head, tail, msg, innov_v, cell_v, anom_v, tang_v, sem):
    pairs = ((innov, innov_v), (cell, cell_v), (anom, anom_v), (tang, tang_v))
    copies = [pltpu.make_async_copy(a, b, sem.at[i]) for i, (a, b) in enumerate(pairs)]
    for c in copies:
        c.start()
    cells = anom_v.shape[0]
    step = 256
    copies[0].wait()
    copies[1].wait()
    ws = []
    for c in range(0, cells, step):
        ids = lax.broadcasted_iota(jnp.int32, (step, 1), 0) + c
        hit = jnp.where(ids == cell_v[...], innov_v[...], 0.0)
        ws.append(jnp.sum(hit, axis=1, keepdims=True))
    copies[2].wait()
    for j, c in enumerate(range(0, cells, step)):
        y = (ws[j] * anom_v[c : c + step].astype(f32)).astype(bf16)
        out[c : c + step] = y
        if c == 0:
            head[...] = y[:BLK]
        if c + step == cells:
            tail[...] = y[step - BLK :]
    lane = lax.broadcasted_iota(jnp.int32, (16, BLK), 1)
    tag = jnp.zeros((16, BLK), f32)
    for i in range(NB):
        tag = jnp.where(lane == i, order[0, i].astype(f32), tag)
    copies[3].wait()
    msg[:COLS] = tang_v[...].astype(bf16)
    msg[COLS:] = tag.astype(bf16)


def local_kernel(scale, before, mid, after, loc, anom, lout, pout, pad):
    n = mid.shape[0]
    pad[:BLK] = before[...]
    pad[BLK : BLK + n] = mid[...]
    pad[BLK + n :] = after[...]
    for b in range(n // BLK):
        left = jnp.concatenate([loc[b, 0], loc[b, 1], loc[b, 2]], axis=1)
        y = jnp.dot(left, pad[b * BLK : b * BLK + 3 * BLK], preferred_element_type=f32)
        lout[b * BLK : (b + 1) * BLK] = y.astype(bf16)
    y = lax.dot_general(lout[...], anom[...], (((0,), (0,)), ((), ())), preferred_element_type=f32)
    pout[...] = (y * scale).astype(bf16)


def other_kernel(scale, lin, near, far, part, pout):
    co = lax.axis_index("co")
    e = lax.axis_index("ens")
    n = near.shape[0]
    half = part.shape[1]
    dims = (((0,), (0,)), ((), ()))
    mine = lin[pl.ds(pl.multiple_of(co * n, n), n), :]
    rest = lin[pl.ds(pl.multiple_of((1 - co) * n, n), n), :]
    y = lax.dot_general(mine, near[...], dims, preferred_element_type=f32)
    y = y + lax.dot_general(rest, far[...], dims, preferred_element_type=f32)
    pout[:, pl.ds(pl.multiple_of(e * half, half), half)] = part[...]
    pout[:, pl.ds(pl.multiple_of((1 - e) * half, half), half)] = (y * scale).astype(bf16)


def map_kernel(own, oth, ords, both, comp, part):
    co = lax.axis_index("co")
    both[co] = own[:COLS]
    both[1 - co] = oth[:COLS]
    lane = lax.broadcasted_iota(jnp.int32, (16, BLK), 1)
    tag = jnp.zeros((16, BLK), f32)
    for i in range(NB):
        tag = jnp.where(lane == i, ords[0, ords[1, i]].astype(f32), tag)
    ys = []
    for i in range(NB):
        low = both[0, pl.ds(pl.multiple_of(ords[1, i] * BLK, BLK), BLK), :]
        y = jnp.dot(both[1, i * BLK : (i + 1) * BLK], low, preferred_element_type=f32)
        ys.append(y.astype(bf16))
    h = COLS // 2
    for i in range(NB):
        comp[i * BLK : (i + 1) * BLK] = ys[i]
    comp[COLS:] = tag.astype(bf16)
    part[:h] = jnp.where(co == 0, jnp.concatenate(ys[: NB // 2], axis=0), jnp.concatenate(ys[NB // 2 :], axis=0))
    part[h:] = tag.astype(bf16)


def arrange_kernel(mine, theirs, tags, maps, table):
    co = lax.axis_index("co")
    z = lax.axis_index("z")
    nz = maps.shape[0]
    h = COLS // 2

    def fill(low, high, tag_low, tag_high):
        for d in range(1, nz // 2):
            for src, tag, k in ((low, tag_low, z + d), (high, tag_high, z + nz - d)):
                k = lax.rem(k, nz)
                maps[k] = src[(d - 1) * MSG : (d - 1) * MSG + COLS]
                for i in range(NB):
                    table[k, i] = tags[tag, d - 1, i]
        k = lax.rem(z + nz // 2, nz)
        at = (nz // 2 - 1) * MSG
        maps[k, :h] = low[at : at + h]
        maps[k, h:] = high[at : at + h]
        for i in range(NB):
            table[k, i] = tags[0, nz // 2 - 1, i]
            table[z, i] = 0

    @pl.when(co == 0)
    def _():
        fill(mine, theirs, 0, 1)

    @pl.when(co == 1)
    def _():
        fill(theirs, mine, 1, 0)


def sum_kernel(parts, own, send):
    co = lax.axis_index("co")
    n, rows, _ = parts.shape
    h = rows // 2
    for place, out in ((co, own), (1 - co, send)):
        at = pl.ds(pl.multiple_of(place * h, h), h)
        y = parts[0, at, :].astype(f32)
        for s in range(1, n):
            y = y + parts[s, at, :].astype(f32)
        out[...] = y.astype(out.dtype)


def apply_forward(src, blocks, order, add):
    xs = [split(src[:, cols_at(order(i))]) for i in range(NB)]
    ys = []
    for i in range(NB):
        y = lax.dot_general(xs[i], blocks(i), (((1,), (1,)), ((), ())), preferred_element_type=f32)
        h = y.shape[0] // 2
        ys.append(y[:h] + y[h:] + add(i))
    return ys


def apply_adjoint(xs, blocks):
    ys = []
    for i in range(NB):
        y = lax.dot_general(split(xs[i]), blocks(i), (((1,), (0,)), ((), ())), preferred_element_type=f32)
        h = y.shape[0] // 2
        ys.append(y[:h] + y[h:])
    return ys


def cut(x, i):
    return x[:, i * BLK : (i + 1) * BLK]


def block_of(both, t):
    return lambda i: both[t, i * BLK : (i + 1) * BLK]


def total_kernel(own, oth, both, ords, out, low, tot, tmp):
    co = lax.axis_index("co")
    z = lax.axis_index("z")
    mine = own[...]
    other = oth[...].astype(f32)
    first = jnp.where(co == 0, mine, other)
    second = jnp.where(co == 0, other, mine)
    low[...] = first
    ys = apply_adjoint([cut(second, i) for i in range(NB)], block_of(both, 1))
    fs = apply_forward(low, block_of(both, 1), lambda i: ords[1, i], lambda i: cut(second, i))
    for i in range(NB):
        tmp[:, cols_at(ords[1, i])] = ys[i]
    back = tmp[...] + first
    ys = apply_adjoint([cut(back, i) for i in range(NB)], block_of(both, 0))
    for i in range(NB):
        tot[:, cols_at(ords[0, i])] = ys[i].astype(bf16)
    adj = tot[...]
    fwd = jnp.concatenate(fs, axis=1).astype(bf16)
    for d in range(out.shape[0]):
        out[d] = jnp.where(d > z, fwd, adj)


def sweep_kernel(recv, maps, tags, both, ords, own, oth, keep, send, st, adj, res):
    co = lax.axis_index("co")
    z = lax.axis_index("z")
    nz = recv.shape[0]
    mine = own[...]
    other = oth[...].astype(f32)
    force = (jnp.where(co == 0, mine, other), jnp.where(co == 0, other, mine))
    st[...] = jnp.where(z > 0, recv[0].astype(f32), 0.0)
    adj[...] = jnp.where(z < nz - 1, recv[nz - 1].astype(f32), 0.0)

    def block(k):
        return lambda i: maps[k, i * BLK : (i + 1) * BLK]

    def forward(k, carry):
        ys = apply_forward(
            st, block(k), lambda i: tags[k, i], lambda i: recv[k, :, i * BLK : (i + 1) * BLK].astype(f32)
        )
        for i in range(NB):
            st[:, i * BLK : (i + 1) * BLK] = ys[i]
        return carry

    def backward(s, carry):
        k = nz - 1 - s
        ys = apply_adjoint([adj[:, i * BLK : (i + 1) * BLK] for i in range(NB)], block(k))
        more = [recv[k, :, cols_at(tags[k, i])].astype(f32) for i in range(NB)]
        for i in range(NB):
            adj[:, cols_at(tags[k, i])] = ys[i] + more[i]
        return carry

    lax.fori_loop(1, z, forward, 0)
    lax.fori_loop(1, nz - 1 - z, backward, 0)
    up = adj[...] + force[1]
    x0 = apply_forward(st, block_of(both, 0), lambda i: ords[0, i], lambda i: cut(force[0], i))
    y1 = apply_adjoint([cut(up, i) for i in range(NB)], block_of(both, 1))
    for i in range(NB):
        res[0, 0, :, i * BLK : (i + 1) * BLK] = x0[i]
    for i in range(NB):
        res[1, 1, :, cols_at(ords[1, i])] = y1[i]
    up = res[1, 1] + force[0]
    x1 = apply_forward(res.at[0, 0], block_of(both, 1), lambda i: ords[1, i], lambda i: cut(force[1], i))
    y0 = apply_adjoint([cut(up, i) for i in range(NB)], block_of(both, 0))
    for i in range(NB):
        res[1, 0, :, i * BLK : (i + 1) * BLK] = x1[i]
    for i in range(NB):
        res[0, 1, :, cols_at(ords[0, i])] = y0[i]
    keep[...] = res[co]
    send[...] = res[1 - co].astype(bf16)


def join_kernel(keep, back, x, y):
    co = lax.axis_index("co")
    h = keep.shape[1]
    for j, out in enumerate((x, y)):
        out[0, pl.ds(pl.multiple_of(co * h, h), h), :] = keep[j]
        out[0, pl.ds(pl.multiple_of((1 - co) * h, h), h), :] = back[j].astype(f32)


def on_device(anomalies, localization, innovations, obs_cell, tangent_blocks, tangent_order):
    cells, half_cols = anomalies.shape
    n_lon = lax.axis_size("lon")
    nz = lax.axis_size("z")
    co = lax.axis_index("co")
    shape = jax.ShapeDtypeStruct
    swap = [(0, 1), (1, 0)]
    scale = float(cells * n_lon) ** (-0.5)

    h = cells // 2
    piece = lax.dynamic_slice_in_dim(anomalies, co * h, h, 0)
    near = lax.ppermute(piece, "ens", swap)

    weighted, head, tail, own_map = call(
        entry_kernel,
        [
            shape((cells, half_cols), bf16),
            shape((BLK, half_cols), bf16),
            shape((BLK, half_cols), bf16),
            shape((MSG, BLK), bf16),
        ],
        [ANY] * 4 + [SM],
        [
            pltpu.VMEM(innovations.shape, f32),
            pltpu.VMEM(obs_cell.shape, jnp.int32),
            pltpu.VMEM(anomalies.shape, bf16),
            pltpu.VMEM((COLS, BLK), f32),
            pltpu.SemaphoreType.DMA((4,)),
        ],
        flops=10**6,
        data=2 * 10**6,
    )(innovations, obs_cell, anomalies, tangent_blocks.reshape(COLS, BLK), tangent_order)
    up = [(i, (i + 1) % n_lon) for i in range(n_lon)]
    down = [(b, a) for a, b in up]
    before = lax.ppermute(tail, "lon", up)
    after = lax.ppermute(head, "lon", down)
    oth_map = lax.ppermute(own_map, "co", swap)

    order_own = tangent_order[0]
    order_oth = oth_map[COLS, :NB].astype(jnp.int32)
    ords = jnp.where(co == 0, jnp.stack([order_own, order_oth]), jnp.stack([order_oth, order_own]))
    both, comp, part = call(
        map_kernel,
        [shape((2, COLS, BLK), bf16), shape((MSG, BLK), bf16), shape((HALF, BLK), bf16)],
        [VM, VM, SM],
        flops=10**7,
        data=2 * 10**6,
    )(own_map, oth_map, ords)
    got = []
    for d in range(1, nz // 2):
        pairs = []
        for k in range(nz):
            pairs.append((((k + d) % nz) * 2, k * 2))
            pairs.append((((k - d) % nz) * 2 + 1, k * 2 + 1))
        got.append(lax.ppermute(comp, ("z", "co"), pairs))
    got.append(lax.ppermute(part, "z", [((k + nz // 2) % nz, k) for k in range(nz)]))

    local, p_own = call(
        functools.partial(local_kernel, scale),
        [shape((cells, half_cols), bf16), shape((half_cols, half_cols), bf16)],
        [VM] * 5,
        [pltpu.VMEM((cells + 2 * BLK, half_cols), bf16)],
        flops=10**9,
        data=4 * 10**6,
    )(before, weighted, after, localization, anomalies)
    far = lax.ppermute(near, "co", swap)
    (p_all,) = call(
        functools.partial(other_kernel, scale), [shape((half_cols, COLS), bf16)], [VM] * 4, flops=10**9, data=3 * 10**6
    )(local, near, far, p_own)
    rows = half_cols // n_lon
    parts = lax.all_to_all(p_all, "lon", 0, 0, tiled=True).reshape(n_lon, rows, COLS)

    hr = rows // 2
    f_own, f_send = call(
        sum_kernel, [shape((hr, COLS), f32), shape((hr, COLS), bf16)], [VM], flops=10**6, data=10**6
    )(parts)
    f_oth = lax.ppermute(f_send, "co", swap)
    (msgs,) = call(
        total_kernel,
        [shape((nz, hr, COLS), bf16)],
        [VM, VM, VM, SM],
        [pltpu.VMEM((hr, COLS), f32), pltpu.VMEM((hr, COLS), bf16), pltpu.VMEM((hr, COLS), f32)],
        flops=10**8,
        data=10**6,
    )(f_own, f_oth, both, ords)
    recv = lax.all_to_all(msgs, "z", 0, 0, tiled=True)

    near_maps = jnp.concatenate(got, axis=0)
    near_maps, msgs = lax.optimization_barrier((near_maps, msgs))
    far_maps = lax.ppermute(near_maps, "co", swap)
    starts = [MSG * j + COLS for j in range(nz // 2 - 1)] + [MSG * (nz // 2 - 1) + COLS // 2]
    tags = jnp.stack([jnp.stack([p[r, :NB] for r in starts]) for p in (near_maps, far_maps)]).astype(jnp.int32)
    maps, table = call(
        arrange_kernel,
        [shape((nz, COLS, BLK), bf16), shape((nz, NB), jnp.int32)],
        [VM, VM, SM],
        flops=10**6,
        data=4 * 10**6,
        specs=[VM, SM],
    )(near_maps, far_maps, tags)
    keep, send = call(
        sweep_kernel,
        [shape((2, hr, COLS), f32), shape((2, hr, COLS), bf16)],
        [VM, VM, SM, VM, SM, VM, VM],
        [
            pltpu.VMEM((hr, COLS), f32),
            pltpu.VMEM((hr, COLS), f32),
            pltpu.VMEM((2, 2, hr, COLS), f32),
        ],
        flops=10**9,
        data=3 * 10**6,
    )(recv, maps, table, both, ords, f_own, f_oth)
    back = lax.ppermute(send, "co", swap)
    x, y = call(join_kernel, [shape((1, rows, COLS), f32)] * 2, [VM] * 2, flops=10**6, data=10**6)(keep, back)
    return x, y


def solution(mesh):
    tm, lon, ens = (mesh.shape[a] for a in ("tm", "lon", "ens"))
    fine = Mesh(mesh.devices.reshape(tm // 2, 2, lon, ens), ("z", "co", "lon", "ens"))
    time = ("z", "co")
    placed = (
        P("lon", "ens"),
        P("lon", None, None, None),
        P(time, "lon"),
        P(time, "lon"),
        P(time, None, None, None),
        P(time, None),
    )
    outs = P(time, ("ens", "lon"), None)

    return jax.shard_map(on_device, mesh=fine, in_specs=placed, out_specs=(outs, outs), check_vma=False)
```

profile of v0, /device:TPU:1, one launch (start us, length us, event | category | flops | bytes accessed | tf_op | source)
XLA Modules:
  0.0 108.9 jit_solution(11941834678554603732)
XLA Ops:
  0.6 0.0 copy-start.1
  0.6 1.2 %constant_dynamic-slice_fusion = bf16[512,512]{1,0:T(8,128)(2,1)S(1)} fusion(bf16[1024,512]{1,0:T(8,128)(2,1)} %anom.3, s32[]{:T(128)S(6)} %select_n.11), kind=kLoop, calls=%fused_computation.6 | loop fusion | bytes 1048580 | tf_op jit(solution)/shard_map/dynamic_slice | solution.py:285
  1.8 3.6 %collective-permute-start.2 = (bf16[512,512]{1,0:T(8,128)(2,1)S(1)}, bf16[512,512]{1,0:T(8,128)(2,1)S(1)}, u32[]{:S(2)}, u32[]{:S(2)}) collective-permute-start(bf16[512,512]{1,0:T(8,128)(2,1)S(1)} %constant_dynamic-slice_fusion), channel_id=1, source_target_pairs={{0,1},{1,0},{2,3},{3,2},{4,5},{5,4},{6,7},{7,6},{8,9},{9,8},{10,11... | collective-permute-start | bytes 1572872 | tf_op jit(solution)/shard_map/ppermute | solution.py:286
  5.5 10.6 %collective-permute-done.2.near = bf16[512,512]{1,0:T(8,128)(2,1)S(1)} collective-permute-done((bf16[512,512]{1,0:T(8,128)(2,1)S(1)}, bf16[512,512]{1,0:T(8,128)(2,1)S(1)}, u32[]{:S(2)}, u32[]{:S(2)}) %collective-permute-start.2) | collective-permute-done | bytes 524320 | tf_op jit(solution)/shard_map/ppermute | solution.py:286
  16.1 2.3 %collective-permute-start.3 = (bf16[512,512]{1,0:T(8,128)(2,1)S(1)}, bf16[512,512]{1,0:T(8,128)(2,1)S(1)}, u32[]{:S(2)}, u32[]{:S(2)}) collective-permute-start(bf16[512,512]{1,0:T(8,128)(2,1)S(1)} %collective-permute-done.2.near), channel_id=1, source_target_pairs={{0,16},{16,0},{1,17},{17,1},{2,18},{18,2},{3,19},{19,3},{4,20},{20... | collective-permute-start | bytes 1572872 | tf_op jit(solution)/shard_map/ppermute | solution.py:340
  18.3 1.2 %copy-done = bf16[1024,512]{1,0:T(8,128)(2,1)S(1)} copy-done((bf16[1024,512]{1,0:T(8,128)(2,1)S(1)}, bf16[1024,512]{1,0:T(8,128)(2,1)}, u32[]{:S(2)}) %copy-start) | copy-done | bytes 1048600
  19.6 1.0 copy-done.2
  20.6 0.7 copy-done.3
  21.3 0.7 copy-done.4
  22.0 0.7 copy-done.5
  22.6 1.2 %shard_map.77 = (bf16[1024,512]{1,0:T(8,128)(2,1)S(1)}, bf16[128,512]{1,0:T(8,128)(2,1)S(1)}, bf16[128,512]{1,0:T(8,128)(2,1)S(1)}, bf16[1040,128]{1,0:T(8,128)(2,1)S(1)}) custom-call(f32[1,512]{1,0:T(1,128)S(1)} %copy-done.3, s32[1,512]{1,0:T(1,128)S(1)} %copy-done.4, bf16[1024,512]{1,0:T(8,128)(2,1)S(1)} %copy-done, f32[1024,128]{1,0:T(8,128)S(1)} %bitcast.6, ...), custom_call_target="tpu_custom_call" | custom-call | flops 1000000 | bytes 2000000 | tf_op jit(solution)/shard_map/pallas_call | solution.py:288
  23.8 1.5 %collective-permute-start = (bf16[128,512]{1,0:T(8,128)(2,1)S(1)}, bf16[128,512]{1,0:T(8,128)(2,1)S(1)}, u32[]{:S(2)}, u32[]{:S(2)}) collective-permute-start(bf16[128,512]{1,0:T(8,128)(2,1)S(1)} %get-tuple-element.18), channel_id=1, source_target_pairs={{0,2},{2,4},{4,6},{6,8},{8,10},{10,12},{12,14},{14,0},{1,3},{3,5},... | collective-permute-start | bytes 393224 | tf_op jit(solution)/shard_map/ppermute | solution.py:309
  25.3 2.5 %collective-permute-start.1 = (bf16[128,512]{1,0:T(8,128)(2,1)S(1)}, bf16[128,512]{1,0:T(8,128)(2,1)S(1)}, u32[]{:S(2)}, u32[]{:S(2)}) collective-permute-start(bf16[128,512]{1,0:T(8,128)(2,1)S(1)} %get-tuple-element.20), channel_id=1, source_target_pairs={{2,0},{4,2},{6,4},{8,6},{10,8},{12,10},{14,12},{0,14},{3,1},{5,3},... | collective-permute-start | bytes 393224 | tf_op jit(solution)/shard_map/ppermute | solution.py:310
  27.9 3.8 %collective-permute-done.before = bf16[128,512]{1,0:T(8,128)(2,1)S(1)} collective-permute-done((bf16[128,512]{1,0:T(8,128)(2,1)S(1)}, bf16[128,512]{1,0:T(8,128)(2,1)S(1)}, u32[]{:S(2)}, u32[]{:S(2)}) %collective-permute-start) | collective-permute-done | bytes 131104 | tf_op jit(solution)/shard_map/ppermute | solution.py:309
  31.7 1.3 %collective-permute-done.1.after = bf16[128,512]{1,0:T(8,128)(2,1)S(1)} collective-permute-done((bf16[128,512]{1,0:T(8,128)(2,1)S(1)}, bf16[128,512]{1,0:T(8,128)(2,1)S(1)}, u32[]{:S(2)}, u32[]{:S(2)}) %collective-permute-start.1) | collective-permute-done | bytes 131104 | tf_op jit(solution)/shard_map/ppermute | solution.py:310
  33.0 1.1 %copy-done.9 = bf16[8,3,128,128]{3,2,1,0:T(8,128)(2,1)S(1)} copy-done((bf16[8,3,128,128]{3,2,1,0:T(8,128)(2,1)S(1)}, bf16[8,3,128,128]{3,2,1,0:T(8,128)(2,1)}, u32[]{:S(2)}) %copy-start.9) | copy-done | bytes 786456
  34.1 1.3 %shard_map.78 = (bf16[1024,512]{1,0:T(8,128)(2,1)S(1)}, bf16[512,512]{1,0:T(8,128)(2,1)S(1)}) custom-call(bf16[128,512]{1,0:T(8,128)(2,1)S(1)} %collective-permute-done.before, bf16[1024,512]{1,0:T(8,128)(2,1)S(1)} %get-tuple-element.19.mid, bf16[128,512]{1,0:T(8,128)(2,1)S(1)} %collective-permute-done.1.after, bf16[8,3,128,128]{3,2,1,0:T(8,128)(2,1)S(1)} %copy-done.9, ...), custom_call_target="tpu_custom_call" | custom-call | flops 1000000000 | bytes 4000000 | tf_op jit(solution)/shard_map/pallas_call | solution.py:332
  35.4 0.0 collective-permute-done.3.far
  35.4 1.7 %shard_map.79 = bf16[512,1024]{1,0:T(8,128)(2,1)} custom-call(bf16[1024,512]{1,0:T(8,128)(2,1)S(1)} %get-tuple-element.21.lin, bf16[512,512]{1,0:T(8,128)(2,1)S(1)} %collective-permute-done.2.near, bf16[512,512]{1,0:T(8,128)(2,1)S(1)} %collective-permute-done.3.far, bf16[512,512]{1,0:T(8,128)(2,1)S(1)} %get-tuple-element.22.part), custom_call_target="tpu_custom_call" | custom-call | flops 1000000000 | bytes 3000000 | tf_op jit(solution)/shard_map/pallas_call | solution.py:341
  37.1 5.0 %all-to-all-start = ((bf16[8,64,1024]{2,1,0:T(8,128)(2,1)}), bf16[8,64,1024]{2,1,0:T(8,128)(2,1)S(1)}, u32[]{:S(2)}, u32[]{:S(2)}) async-start(bf16[8,64,1024]{2,1,0:T(8,128)(2,1)} %bitcast.1), calls=%async_computation | async-start | bytes 2097152 | tf_op jit(solution)/shard_map/all_to_all | solution.py:345
  42.1 1.1 %collective-permute-start.5 = (bf16[1040,128]{1,0:T(8,128)(2,1)S(1)}, bf16[1040,128]{1,0:T(8,128)(2,1)S(1)}, u32[]{:S(2)}, u32[]{:S(2)}) collective-permute-start(bf16[1040,128]{1,0:T(8,128)(2,1)S(1)} %get-tuple-element.25.own), channel_id=1, source_target_pairs={{0,16},{16,0},{1,17},{17,1},{2,18},{18,2},{3,19},{19,3},{4,20},{20... | collective-permute-start | bytes 798728 | tf_op jit(solution)/shard_map/ppermute | solution.py:311
  43.2 1.2 %collective-permute-done.5.oth = bf16[1040,128]{1,0:T(8,128)(2,1)S(1)} collective-permute-done((bf16[1040,128]{1,0:T(8,128)(2,1)S(1)}, bf16[1040,128]{1,0:T(8,128)(2,1)S(1)}, u32[]{:S(2)}, u32[]{:S(2)}) %collective-permute-start.5) | collective-permute-done | bytes 266272 | tf_op jit(solution)/shard_map/ppermute | solution.py:311
  44.4 0.8 shard_map.81
  45.3 4.4 %collective-permute-start.8 = (bf16[1040,128]{1,0:T(8,128)(2,1)S(1)}, bf16[1040,128]{1,0:T(8,128)(2,1)S(1)}, u32[]{:S(2)}, u32[]{:S(2)}) collective-permute-start(bf16[1040,128]{1,0:T(8,128)(2,1)S(1)} %get-tuple-element.27), channel_id=1, source_target_pairs={{96,0},{176,16},{128,32},{208,48},{160,64},{240,80},{192,96},{16,1... | collective-permute-start | bytes 798728 | tf_op jit(solution)/shard_map/ppermute | solution.py:329
  49.7 3.3 %collective-permute-start.7 = (bf16[1040,128]{1,0:T(8,128)(2,1)S(1)}, bf16[1040,128]{1,0:T(8,128)(2,1)S(1)}, u32[]{:S(2)}, u32[]{:S(2)}) collective-permute-start(bf16[1040,128]{1,0:T(8,128)(2,1)S(1)} %get-tuple-element.27), channel_id=1, source_target_pairs={{64,0},{208,16},{96,32},{240,48},{128,64},{16,80},{160,96},{48,112... | collective-permute-start | bytes 798728 | tf_op jit(solution)/shard_map/ppermute | solution.py:329
  53.0 0.7 collective-permute-start.6
  53.7 0.5 collective-permute-start.9
  54.3 2.2 %all-to-all-done.parts = bf16[8,64,1024]{2,1,0:T(8,128)(2,1)S(1)} async-done(((bf16[8,64,1024]{2,1,0:T(8,128)(2,1)}), bf16[8,64,1024]{2,1,0:T(8,128)(2,1)S(1)}, u32[]{:S(2)}, u32[]{:S(2)}) %all-to-all-start) | async-done | bytes 1048608 | tf_op jit(solution)/shard_map/all_to_all | solution.py:345
  56.5 0.1 shard_map.80
  56.6 2.4 %collective-permute-start.4 = (bf16[32,1024]{1,0:T(8,128)(2,1)S(1)}, bf16[32,1024]{1,0:T(8,128)(2,1)S(1)}, u32[]{:S(2)}, u32[]{:S(2)}) collective-permute-start(bf16[32,1024]{1,0:T(8,128)(2,1)S(1)} %get-tuple-element.24), channel_id=1, source_target_pairs={{0,16},{16,0},{1,17},{17,1},{2,18},{18,2},{3,19},{19,3},{4,20},{20... | collective-permute-start | bytes 196616 | tf_op jit(solution)/shard_map/ppermute | solution.py:351
  59.0 17.4 %collective-permute-done.9 = bf16[528,128]{1,0:T(8,128)(2,1)S(1)} collective-permute-done((bf16[528,128]{1,0:T(8,128)(2,1)S(1)}, bf16[528,128]{1,0:T(8,128)(2,1)S(1)}, u32[]{:S(2)}, u32[]{:S(2)}) %collective-permute-start.9) | collective-permute-done | bytes 135200 | tf_op jit(solution)/shard_map/ppermute | solution.py:330
  76.4 0.0 collective-permute-done.8
  76.4 0.0 collective-permute-done.7
  76.4 0.0 collective-permute-done.6
  76.4 0.1 pad_maximum_fusion.mine
  76.5 0.0 collective-permute-done.4.oth
  76.5 1.9 %shard_map.82 = bf16[8,32,1024]{2,1,0:T(8,128)(2,1)} custom-call(f32[32,1024]{1,0:T(8,128)S(1)} %get-tuple-element.23.own, bf16[32,1024]{1,0:T(8,128)(2,1)S(1)} %collective-permute-done.4.oth, bf16[2,1024,128]{2,1,0:T(8,128)(2,1)S(1)} %get-tuple-element.26.both, s32[2,8]{1,0:T(2,128)S(1)} %add_select_fusion.ords), custom_call_target="tpu_custom_call" | custom-call | flops 100000000 | bytes 1000000 | tf_op jit(solution)/shard_map/pallas_call | solution.py:352
  78.3 0.1 collective-permute-start.10
  78.4 5.8 %all-to-all-start.1 = ((bf16[8,32,1024]{2,1,0:T(8,128)(2,1)}), bf16[8,32,1024]{2,1,0:T(8,128)(2,1)S(1)}, u32[]{:S(2)}, u32[]{:S(2)}) async-start(bf16[8,32,1024]{2,1,0:T(8,128)(2,1)} %shard_map.82), calls=%async_computation.1 | async-start | bytes 1048576 | tf_op jit(solution)/shard_map/all_to_all | solution.py:360
  84.3 0.0 collective-permute-done.10.theirs
  84.3 1.4 %shard_map.83 = (bf16[8,1024,128]{2,1,0:T(8,128)(2,1)S(1)}, s32[8,8]{1,0:T(8,128)S(1)}) custom-call(bf16[3648,128]{1,0:T(8,128)(2,1)S(1)} %pad_maximum_fusion.mine, bf16[3648,128]{1,0:T(8,128)(2,1)S(1)} %collective-permute-done.10.theirs, s32[2,4,8]{2,1,0:T(4,128)S(1)} %maximum_convert_fusion.tags), custom_call_target="tpu_custom_call" | custom-call | flops 1000000 | bytes 4000000 | tf_op jit(solution)/shard_map/pallas_call | solution.py:367
  85.8 1.3 %copy-done.7 = bf16[8,1024,128]{2,1,0:T(8,128)(2,1)} copy-done((bf16[8,1024,128]{2,1,0:T(8,128)(2,1)}, bf16[8,1024,128]{2,1,0:T(8,128)(2,1)S(1)}, u32[]{:S(2)}) %copy-start.7) | copy-done | bytes 2097176
  87.1 15.2 %all-to-all-done.1.recv = bf16[8,32,1024]{2,1,0:T(8,128)(2,1)S(1)} async-done(((bf16[8,32,1024]{2,1,0:T(8,128)(2,1)}), bf16[8,32,1024]{2,1,0:T(8,128)(2,1)S(1)}, u32[]{:S(2)}, u32[]{:S(2)}) %all-to-all-start.1) | async-done | bytes 524320 | tf_op jit(solution)/shard_map/all_to_all | solution.py:360
  102.3 1.6 %copy-done.8 = bf16[8,1024,128]{2,1,0:T(8,128)(2,1)S(1)} copy-done((bf16[8,1024,128]{2,1,0:T(8,128)(2,1)S(1)}, bf16[8,1024,128]{2,1,0:T(8,128)(2,1)}, u32[]{:S(2)}) %copy-start.8) | copy-done | bytes 2097176
  103.9 2.7 %shard_map.84 = (f32[2,32,1024]{2,1,0:T(8,128)S(1)}, bf16[2,32,1024]{2,1,0:T(8,128)(2,1)S(1)}) custom-call(bf16[8,32,1024]{2,1,0:T(8,128)(2,1)S(1)} %all-to-all-done.1.recv, bf16[8,1024,128]{2,1,0:T(8,128)(2,1)S(1)} %copy-done.8, s32[8,8]{1,0:T(8,128)S(1)} %get-tuple-element.31.tags, bf16[2,1024,128]{2,1,0:T(8,128)(2,1)S(1)} %get-tuple-element.26.both, ...), custom_call_target="tpu_custom_call" | custom-call | flops 1000000000 | bytes 3000000 | tf_op jit(solution)/shard_map/pallas_call | solution.py:375
  106.6 0.5 collective-permute-start.11
  107.1 1.0 collective-permute-done.11.back
  108.1 0.8 shard_map.85
  (18 shorter events, 0.1 us)
Async XLA Ops:
  0.6 32.4 %copy-start.1 = (bf16[1024,512]{1,0:T(8,128)(2,1)S(1)}, bf16[1024,512]{1,0:T(8,128)(2,1)}, u32[]{:S(2)}) copy-start(bf16[1024,512]{1,0:T(8,128)(2,1)} %anom.3) | copy-start | bytes 3145732
  1.8 14.3 %collective-permute-start.2 = (bf16[512,512]{1,0:T(8,128)(2,1)S(1)}, bf16[512,512]{1,0:T(8,128)(2,1)S(1)}, u32[]{:S(2)}, u32[]{:S(2)}) collective-permute-start(bf16[512,512]{1,0:T(8,128)(2,1)S(1)} %constant_dynamic-slice_fusion), channel_id=1, source_target_pairs={{0,1},{1,0},{2,3},{3,2},{4,5},{5,4},{6,7},{7,6},{8,9},{9,8},{10,11... | collective-permute-start | bytes 1572872 | tf_op jit(solution)/shard_map/ppermute | solution.py:286
  16.1 19.3 %collective-permute-start.3 = (bf16[512,512]{1,0:T(8,128)(2,1)S(1)}, bf16[512,512]{1,0:T(8,128)(2,1)S(1)}, u32[]{:S(2)}, u32[]{:S(2)}) collective-permute-start(bf16[512,512]{1,0:T(8,128)(2,1)S(1)} %collective-permute-done.2.near), channel_id=1, source_target_pairs={{0,16},{16,0},{1,17},{17,1},{2,18},{18,2},{3,19},{19,3},{4,20},{20... | collective-permute-start | bytes 1572872 | tf_op jit(solution)/shard_map/ppermute | solution.py:340
  18.3 1.2 %copy-start = (bf16[1024,512]{1,0:T(8,128)(2,1)S(1)}, bf16[1024,512]{1,0:T(8,128)(2,1)}, u32[]{:S(2)}) copy-start(bf16[1024,512]{1,0:T(8,128)(2,1)} %anom.3) | copy-start | bytes 3145732
  19.6 1.0 copy-start.2
  20.6 0.7 copy-start.3
  21.3 0.7 copy-start.4
  22.0 0.7 copy-start.5
  23.8 7.8 %collective-permute-start = (bf16[128,512]{1,0:T(8,128)(2,1)S(1)}, bf16[128,512]{1,0:T(8,128)(2,1)S(1)}, u32[]{:S(2)}, u32[]{:S(2)}) collective-permute-start(bf16[128,512]{1,0:T(8,128)(2,1)S(1)} %get-tuple-element.18), channel_id=1, source_target_pairs={{0,2},{2,4},{4,6},{6,8},{8,10},{10,12},{12,14},{14,0},{1,3},{3,5},... | collective-permute-start | bytes 393224 | tf_op jit(solution)/shard_map/ppermute | solution.py:309
  25.3 7.7 %collective-permute-start.1 = (bf16[128,512]{1,0:T(8,128)(2,1)S(1)}, bf16[128,512]{1,0:T(8,128)(2,1)S(1)}, u32[]{:S(2)}, u32[]{:S(2)}) collective-permute-start(bf16[128,512]{1,0:T(8,128)(2,1)S(1)} %get-tuple-element.20), channel_id=1, source_target_pairs={{2,0},{4,2},{6,4},{8,6},{10,8},{12,10},{14,12},{0,14},{3,1},{5,3},... | collective-permute-start | bytes 393224 | tf_op jit(solution)/shard_map/ppermute | solution.py:310
  33.0 1.1 %copy-start.9 = (bf16[8,3,128,128]{3,2,1,0:T(8,128)(2,1)S(1)}, bf16[8,3,128,128]{3,2,1,0:T(8,128)(2,1)}, u32[]{:S(2)}) copy-start(bf16[8,3,128,128]{3,2,1,0:T(8,128)(2,1)} %loc.1) | copy-start | bytes 2359300
  37.1 7.3 %copy-start.6 = (s32[1,8]{1,0:T(1,128)S(1)}, s32[1,8]{1,0:T(1,128)}, u32[]{:S(2)}) copy-start(s32[1,8]{1,0:T(1,128)} %order.1) | copy-start | bytes 100
  37.1 19.3 %all-to-all-start = ((bf16[8,64,1024]{2,1,0:T(8,128)(2,1)}), bf16[8,64,1024]{2,1,0:T(8,128)(2,1)S(1)}, u32[]{:S(2)}, u32[]{:S(2)}) async-start(bf16[8,64,1024]{2,1,0:T(8,128)(2,1)} %bitcast.1), calls=%async_computation | async-start | bytes 2097152 | tf_op jit(solution)/shard_map/all_to_all | solution.py:345
  42.1 2.3 %collective-permute-start.5 = (bf16[1040,128]{1,0:T(8,128)(2,1)S(1)}, bf16[1040,128]{1,0:T(8,128)(2,1)S(1)}, u32[]{:S(2)}, u32[]{:S(2)}) collective-permute-start(bf16[1040,128]{1,0:T(8,128)(2,1)S(1)} %get-tuple-element.25.own), channel_id=1, source_target_pairs={{0,16},{16,0},{1,17},{17,1},{2,18},{18,2},{3,19},{19,3},{4,20},{20... | collective-permute-start | bytes 798728 | tf_op jit(solution)/shard_map/ppermute | solution.py:311
  45.3 31.1 %collective-permute-start.8 = (bf16[1040,128]{1,0:T(8,128)(2,1)S(1)}, bf16[1040,128]{1,0:T(8,128)(2,1)S(1)}, u32[]{:S(2)}, u32[]{:S(2)}) collective-permute-start(bf16[1040,128]{1,0:T(8,128)(2,1)S(1)} %get-tuple-element.27), channel_id=1, source_target_pairs={{96,0},{176,16},{128,32},{208,48},{160,64},{240,80},{192,96},{16,1... | collective-permute-start | bytes 798728 | tf_op jit(solution)/shard_map/ppermute | solution.py:329
  49.7 26.7 %collective-permute-start.7 = (bf16[1040,128]{1,0:T(8,128)(2,1)S(1)}, bf16[1040,128]{1,0:T(8,128)(2,1)S(1)}, u32[]{:S(2)}, u32[]{:S(2)}) collective-permute-start(bf16[1040,128]{1,0:T(8,128)(2,1)S(1)} %get-tuple-element.27), channel_id=1, source_target_pairs={{64,0},{208,16},{96,32},{240,48},{128,64},{16,80},{160,96},{48,112... | collective-permute-start | bytes 798728 | tf_op jit(solution)/shard_map/ppermute | solution.py:329
  53.0 23.4 %collective-permute-start.6 = (bf16[1040,128]{1,0:T(8,128)(2,1)S(1)}, bf16[1040,128]{1,0:T(8,128)(2,1)S(1)}, u32[]{:S(2)}, u32[]{:S(2)}) collective-permute-start(bf16[1040,128]{1,0:T(8,128)(2,1)S(1)} %get-tuple-element.27), channel_id=1, source_target_pairs={{32,0},{240,16},{64,32},{16,48},{96,64},{48,80},{128,96},{80,112},... | collective-permute-start | bytes 798728 | tf_op jit(solution)/shard_map/ppermute | solution.py:329
  53.7 22.7 %collective-permute-start.9 = (bf16[528,128]{1,0:T(8,128)(2,1)S(1)}, bf16[528,128]{1,0:T(8,128)(2,1)S(1)}, u32[]{:S(2)}, u32[]{:S(2)}) collective-permute-start(bf16[528,128]{1,0:T(8,128)(2,1)S(1)} %get-tuple-element.28), channel_id=1, source_target_pairs={{128,0},{160,32},{192,64},{224,96},{0,128},{32,160},{64,192},{96,2... | collective-permute-start | bytes 405512 | tf_op jit(solution)/shard_map/ppermute | solution.py:330
  56.6 19.9 %collective-permute-start.4 = (bf16[32,1024]{1,0:T(8,128)(2,1)S(1)}, bf16[32,1024]{1,0:T(8,128)(2,1)S(1)}, u32[]{:S(2)}, u32[]{:S(2)}) collective-permute-start(bf16[32,1024]{1,0:T(8,128)(2,1)S(1)} %get-tuple-element.24), channel_id=1, source_target_pairs={{0,16},{16,0},{1,17},{17,1},{2,18},{18,2},{3,19},{19,3},{4,20},{20... | collective-permute-start | bytes 196616 | tf_op jit(solution)/shard_map/ppermute | solution.py:351
  78.3 5.9 %collective-permute-start.10 = (bf16[3648,128]{1,0:T(8,128)(2,1)S(1)}, bf16[3648,128]{1,0:T(8,128)(2,1)S(1)}, u32[]{:S(2)}, u32[]{:S(2)}) collective-permute-start(bf16[3648,128]{1,0:T(8,128)(2,1)S(1)} %pad_maximum_fusion.mine), channel_id=1, source_target_pairs={{0,16},{16,0},{1,17},{17,1},{2,18},{18,2},{3,19},{19,3},{4,20},{20... | collective-permute-start | bytes 2801672 | tf_op jit(solution)/shard_map/ppermute | solution.py:364
  78.4 23.9 %all-to-all-start.1 = ((bf16[8,32,1024]{2,1,0:T(8,128)(2,1)}), bf16[8,32,1024]{2,1,0:T(8,128)(2,1)S(1)}, u32[]{:S(2)}, u32[]{:S(2)}) async-start(bf16[8,32,1024]{2,1,0:T(8,128)(2,1)} %shard_map.82), calls=%async_computation.1 | async-start | bytes 1048576 | tf_op jit(solution)/shard_map/all_to_all | solution.py:360
  85.8 1.4 %copy-start.7 = (bf16[8,1024,128]{2,1,0:T(8,128)(2,1)}, bf16[8,1024,128]{2,1,0:T(8,128)(2,1)S(1)}, u32[]{:S(2)}) copy-start(bf16[8,1024,128]{2,1,0:T(8,128)(2,1)S(1)} %get-tuple-element.30.maps) | copy-start | bytes 6291460
  102.3 1.6 %copy-start.8 = (bf16[8,1024,128]{2,1,0:T(8,128)(2,1)S(1)}, bf16[8,1024,128]{2,1,0:T(8,128)(2,1)}, u32[]{:S(2)}) copy-start(bf16[8,1024,128]{2,1,0:T(8,128)(2,1)} %copy-done.7) | copy-start | bytes 6291460
  106.6 1.5 %collective-permute-start.11 = (bf16[2,32,1024]{2,1,0:T(8,128)(2,1)S(1)}, bf16[2,32,1024]{2,1,0:T(8,128)(2,1)S(1)}, u32[]{:S(2)}, u32[]{:S(2)}) collective-permute-start(bf16[2,32,1024]{2,1,0:T(8,128)(2,1)S(1)} %get-tuple-element.33), channel_id=1, source_target_pairs={{0,16},{16,0},{1,17},{17,1},{2,18},{18,2},{3,19},{19,3},{4,20},{20... | collective-permute-start | bytes 393224 | tf_op jit(solution)/shard_map/ppermute | solution.py:387
where the time goes:
time: 109 us
  waiting for transfers between devices  52.6 us (48%)
  starting transfers between devices  33.9 us (31%)
  Pallas kernels  11.9 us (11%)
  local copies, waits for them, and re-layouts  9.54 us (9%)
    ppermute x1, waiting for transfers between devices, on_device(): lax.ppermute(part, 'z', [((k + nz // 2) % nz, k) for k in range(nz)])  17.4 us
    all_to_all x1, waiting for transfers between devices, on_device(): recv = lax.all_to_all(msgs, 'z', 0, 0, tiled=True)  15.2 us
    ppermute x1, waiting for transfers between devices, on_device(): near = lax.ppermute(piece, 'ens', swap)  10.6 us
    ppermute x3, starting transfers between devices, on_device(): got.append(lax.ppermute(comp, ('z', 'co'), pairs))  8.45 us
    unnamed x20, local copies, waits for them, and re-layouts  8.37 us
    all_to_all x1, starting transfers between devices, on_device(): recv = lax.all_to_all(msgs, 'z', 0, 0, tiled=True)  5.83 us
    all_to_all x1, starting transfers between devices, on_device(): lax.all_to_all(p_all, 'lon', 0, 0, tiled=True).reshape(n_lon, rows, COLS)  4.96 us
    ppermute x1, waiting for transfers between devices, on_device(): before = lax.ppermute(tail, 'lon', up)  3.78 us
  transfers between devices with their start and end apart: 14, of which 8 were waited for; matrix products, arithmetic and copies ran while one was open for 0% of the time, Pallas kernels for 4%

commit v1 on v0

--- a/solution.py
+++ b/solution.py
@@ -16,15 +16,14 @@
 
 VM = pl.BlockSpec(memory_space=pltpu.VMEM)
 SM = pl.BlockSpec(memory_space=pltpu.SMEM)
-ANY = pl.BlockSpec(memory_space=pl.ANY)
+HBM = pl.BlockSpec(memory_space=pltpu.HBM)
 
 MSG = COLS + 16
-HALF = COLS // 2 + 16
 MIB = 1024 * 1024
 
 
 def call(kernel, outs, ins, scratch=(), flops=0, data=0, grant=16, specs=None):
-    return pl.pallas_call(
+    made = pl.pallas_call(
         kernel,
         out_shape=outs,
         in_specs=ins,
@@ -34,6 +33,12 @@
         cost_estimate=pl.CostEstimate(flops=flops, bytes_accessed=data, transcendentals=0),
     )
 
+    def run(*args):
+        args = [pltpu.with_memory_space_constraint(a, pltpu.HBM) if i is HBM else a for a, i in zip(args, ins)]
+        return made(*args)
+
+    return run
+
 
 def split(x):
     hi = x.astype(bf16)
@@ -45,45 +50,73 @@
     return pl.ds(pl.multiple_of(i * BLK, BLK), BLK)
 
 
-def entry_kernel(innov, cell, anom, tang, order, out, head, tail, msg, innov_v, cell_v, anom_v, tang_v, sem):
-    pairs = ((innov, innov_v), (cell, cell_v), (anom, anom_v), (tang, tang_v))
+def weights(cell, innov, start, count):
+    ids = lax.broadcasted_iota(jnp.int32, (count, 1), 0) + start
+    return jnp.sum(jnp.where(ids == cell[...], innov[...], 0.0), axis=1, keepdims=True)
+
+
+def entry_kernel(innov, cell, anom, tang, order, head, tail, piece, msg, innov_v, cell_v, edge, tang_v, order_s, sem):
+    co = lax.axis_index("co")
+    cells = anom.shape[0]
+    h = piece.shape[0]
+    pairs = (
+        (innov, innov_v),
+        (cell, cell_v),
+        (anom.at[pl.ds(0, BLK)], edge.at[0]),
+        (anom.at[pl.ds(cells - BLK, BLK)], edge.at[1]),
+        (tang, tang_v),
+        (anom.at[pl.ds(pl.multiple_of(co * h, h), h)], piece),
+        (order, order_s),
+    )
     copies = [pltpu.make_async_copy(a, b, sem.at[i]) for i, (a, b) in enumerate(pairs)]
     for c in copies:
         c.start()
-    cells = anom_v.shape[0]
-    step = 256
     copies[0].wait()
     copies[1].wait()
-    ws = []
-    for c in range(0, cells, step):
-        ids = lax.broadcasted_iota(jnp.int32, (step, 1), 0) + c
-        hit = jnp.where(ids == cell_v[...], innov_v[...], 0.0)
-        ws.append(jnp.sum(hit, axis=1, keepdims=True))
+    w0 = weights(cell_v, innov_v, 0, BLK)
+    w1 = weights(cell_v, innov_v, cells - BLK, BLK)
+    copies[2].wait()
+    copies[3].wait()
+    head[...] = (w0 * edge[0].astype(f32)).astype(bf16)
+    tail[...] = (w1 * edge[1].astype(f32)).astype(bf16)
+    copies[6].wait()
+    lane = lax.broadcasted_iota(jnp.int32, (16, BLK), 1)
+    tag = jnp.zeros((16, BLK), f32)
+    for i in range(NB):
+        tag = jnp.where(lane == i, order_s[0, i].astype(f32), tag)
+    msg[COLS:] = tag.astype(bf16)
+    copies[4].wait()
+    msg[:COLS] = tang_v[...].astype(bf16)
+    copies[5].wait()
+
+
+def inner_kernel(innov, cell, anom, loc, out, anom_v, loc_v, innov_v, cell_v, sem):
+    pairs = ((innov, innov_v), (cell, cell_v), (anom, anom_v), (loc, loc_v))
+    copies = [pltpu.make_async_copy(a, b, sem.at[i]) for i, (a, b) in enumerate(pairs)]
+    for c in copies:
+        c.start()
+    copies[0].wait()
+    copies[1].wait()
+    cells = out.shape[0]
+    step = 256
+    ws = [weights(cell_v, innov_v, c, step) for c in range(0, cells, step)]
     copies[2].wait()
     for j, c in enumerate(range(0, cells, step)):
-        y = (ws[j] * anom_v[c : c + step].astype(f32)).astype(bf16)
-        out[c : c + step] = y
-        if c == 0:
-            head[...] = y[:BLK]
-        if c + step == cells:
-            tail[...] = y[step - BLK :]
-    lane = lax.broadcasted_iota(jnp.int32, (16, BLK), 1)
-    tag = jnp.zeros((16, BLK), f32)
-    for i in range(NB):
-        tag = jnp.where(lane == i, order[0, i].astype(f32), tag)
+        out[c : c + step] = (ws[j] * anom_v[c : c + step].astype(f32)).astype(bf16)
     copies[3].wait()
-    msg[:COLS] = tang_v[...].astype(bf16)
-    msg[COLS:] = tag.astype(bf16)
-
-
-def local_kernel(scale, before, mid, after, loc, anom, lout, pout, pad):
-    n = mid.shape[0]
-    pad[:BLK] = before[...]
-    pad[BLK : BLK + n] = mid[...]
-    pad[BLK + n :] = after[...]
-    for b in range(n // BLK):
+
+
+def local_kernel(scale, before, mid, after, loc, anom, lout, pout):
+    n = mid.shape[0] // BLK
+    for b in range(n):
         left = jnp.concatenate([loc[b, 0], loc[b, 1], loc[b, 2]], axis=1)
-        y = jnp.dot(left, pad[b * BLK : b * BLK + 3 * BLK], preferred_element_type=f32)
+        if b == 0:
+            right = jnp.concatenate([before[...], mid[: 2 * BLK]], axis=0)
+        elif b == n - 1:
+            right = jnp.concatenate([mid[(b - 1) * BLK :], after[...]], axis=0)
+        else:
+            right = mid[(b - 1) * BLK : (b + 2) * BLK]
+        y = jnp.dot(left, right, preferred_element_type=f32)
         lout[b * BLK : (b + 1) * BLK] = y.astype(bf16)
     y = lax.dot_general(lout[...], anom[...], (((0,), (0,)), ((), ())), preferred_element_type=f32)
     pout[...] = (y * scale).astype(bf16)
@@ -103,55 +136,43 @@
     pout[:, pl.ds(pl.multiple_of((1 - e) * half, half), half)] = (y * scale).astype(bf16)
 
 
-def map_kernel(own, oth, ords, both, comp, part):
+def map_kernel(own, oth, both, comp, ords, ints, sem):
     co = lax.axis_index("co")
     both[co] = own[:COLS]
     both[1 - co] = oth[:COLS]
+    mine = own[COLS:].astype(f32)[:8].astype(jnp.int32)
+    other = oth[COLS:].astype(f32)[:8].astype(jnp.int32)
+    row = lax.broadcasted_iota(jnp.int32, (8, BLK), 0)
+    ints[...] = jnp.where(row == co, mine, other)
+    c = pltpu.make_async_copy(ints, ords, sem)
+    c.start()
+    c.wait()
     lane = lax.broadcasted_iota(jnp.int32, (16, BLK), 1)
     tag = jnp.zeros((16, BLK), f32)
     for i in range(NB):
         tag = jnp.where(lane == i, ords[0, ords[1, i]].astype(f32), tag)
-    ys = []
     for i in range(NB):
         low = both[0, pl.ds(pl.multiple_of(ords[1, i] * BLK, BLK), BLK), :]
         y = jnp.dot(both[1, i * BLK : (i + 1) * BLK], low, preferred_element_type=f32)
-        ys.append(y.astype(bf16))
-    h = COLS // 2
-    for i in range(NB):
-        comp[i * BLK : (i + 1) * BLK] = ys[i]
+        comp[i * BLK : (i + 1) * BLK] = y.astype(bf16)
     comp[COLS:] = tag.astype(bf16)
-    part[:h] = jnp.where(co == 0, jnp.concatenate(ys[: NB // 2], axis=0), jnp.concatenate(ys[NB // 2 :], axis=0))
-    part[h:] = tag.astype(bf16)
-
-
-def arrange_kernel(mine, theirs, tags, maps, table):
+
+
+def arrange_kernel(*refs):
+    *got, maps, table, ints, sem = refs
     co = lax.axis_index("co")
     z = lax.axis_index("z")
     nz = maps.shape[0]
-    h = COLS // 2
-
-    def fill(low, high, tag_low, tag_high):
-        for d in range(1, nz // 2):
-            for src, tag, k in ((low, tag_low, z + d), (high, tag_high, z + nz - d)):
-                k = lax.rem(k, nz)
-                maps[k] = src[(d - 1) * MSG : (d - 1) * MSG + COLS]
-                for i in range(NB):
-                    table[k, i] = tags[tag, d - 1, i]
-        k = lax.rem(z + nz // 2, nz)
-        at = (nz // 2 - 1) * MSG
-        maps[k, :h] = low[at : at + h]
-        maps[k, h:] = high[at : at + h]
-        for i in range(NB):
-            table[k, i] = tags[0, nz // 2 - 1, i]
-            table[z, i] = 0
-
-    @pl.when(co == 0)
-    def _():
-        fill(mine, theirs, 0, 1)
-
-    @pl.when(co == 1)
-    def _():
-        fill(theirs, mine, 1, 0)
+    for j, src in enumerate(got):
+        d = j + 1 if j < nz // 2 else j + 1 - nz // 2
+        back = co == 0 if j < nz // 2 else co == 1
+        k = lax.rem(jnp.where(back, z + nz - d, z + d), nz)
+        maps[k] = src[:COLS]
+        ints[pl.ds(k, 1), :] = src[COLS:].astype(f32)[:1].astype(jnp.int32)
+    ints[pl.ds(z, 1), :] = jnp.zeros((1, BLK), jnp.int32)
+    c = pltpu.make_async_copy(ints, table, sem)
+    c.start()
+    c.wait()
 
 
 def sum_kernel(parts, own, send):
@@ -215,10 +236,21 @@
         out[d] = jnp.where(d > z, fwd, adj)
 
 
-def sweep_kernel(recv, maps, tags, both, ords, own, oth, keep, send, st, adj, res):
+def sweep_kernel(recv, stored, tags, both, ords, own, oth, keep, send, maps, st, adj, res, sem):
     co = lax.axis_index("co")
     z = lax.axis_index("z")
     nz = recv.shape[0]
+
+    def copy(k):
+        return pltpu.make_async_copy(stored.at[k], maps.at[k], sem.at[k])
+
+    for j in range(1, nz // 2):
+        for k in (j, nz - 1 - j):
+
+            @pl.when(k != z)
+            def _():
+                copy(k).start()
+
     mine = own[...]
     other = oth[...].astype(f32)
     force = (jnp.where(co == 0, mine, other), jnp.where(co == 0, other, mine))
@@ -229,6 +261,7 @@
         return lambda i: maps[k, i * BLK : (i + 1) * BLK]
 
     def forward(k, carry):
+        copy(k).wait()
         ys = apply_forward(
             st, block(k), lambda i: tags[k, i], lambda i: recv[k, :, i * BLK : (i + 1) * BLK].astype(f32)
         )
@@ -238,6 +271,7 @@
 
     def backward(s, carry):
         k = nz - 1 - s
+        copy(k).wait()
         ys = apply_adjoint([adj[:, i * BLK : (i + 1) * BLK] for i in range(NB)], block(k))
         more = [recv[k, :, cols_at(tags[k, i])].astype(f32) for i in range(NB)]
         for i in range(NB):
@@ -276,67 +310,71 @@
     cells, half_cols = anomalies.shape
     n_lon = lax.axis_size("lon")
     nz = lax.axis_size("z")
-    co = lax.axis_index("co")
     shape = jax.ShapeDtypeStruct
     swap = [(0, 1), (1, 0)]
     scale = float(cells * n_lon) ** (-0.5)
 
-    h = cells // 2
-    piece = lax.dynamic_slice_in_dim(anomalies, co * h, h, 0)
-    near = lax.ppermute(piece, "ens", swap)
-
-    weighted, head, tail, own_map = call(
+    head, tail, piece, own_map = call(
         entry_kernel,
         [
-            shape((cells, half_cols), bf16),
             shape((BLK, half_cols), bf16),
             shape((BLK, half_cols), bf16),
+            shape((cells // 2, half_cols), bf16),
             shape((MSG, BLK), bf16),
         ],
-        [ANY] * 4 + [SM],
+        [HBM] * 5,
         [
             pltpu.VMEM(innovations.shape, f32),
             pltpu.VMEM(obs_cell.shape, jnp.int32),
-            pltpu.VMEM(anomalies.shape, bf16),
+            pltpu.VMEM((2, BLK, half_cols), bf16),
             pltpu.VMEM((COLS, BLK), f32),
-            pltpu.SemaphoreType.DMA((4,)),
+            pltpu.SMEM(tangent_order.shape, jnp.int32),
+            pltpu.SemaphoreType.DMA((7,)),
         ],
         flops=10**6,
         data=2 * 10**6,
     )(innovations, obs_cell, anomalies, tangent_blocks.reshape(COLS, BLK), tangent_order)
     up = [(i, (i + 1) % n_lon) for i in range(n_lon)]
     down = [(b, a) for a, b in up]
+    near = lax.ppermute(piece, "ens", swap)
     before = lax.ppermute(tail, "lon", up)
     after = lax.ppermute(head, "lon", down)
     oth_map = lax.ppermute(own_map, "co", swap)
 
-    order_own = tangent_order[0]
-    order_oth = oth_map[COLS, :NB].astype(jnp.int32)
-    ords = jnp.where(co == 0, jnp.stack([order_own, order_oth]), jnp.stack([order_oth, order_own]))
-    both, comp, part = call(
+    both, comp, ords = call(
         map_kernel,
-        [shape((2, COLS, BLK), bf16), shape((MSG, BLK), bf16), shape((HALF, BLK), bf16)],
-        [VM, VM, SM],
+        [shape((2, COLS, BLK), bf16), shape((MSG, BLK), bf16), shape((8, BLK), jnp.int32)],
+        [VM, VM],
+        [pltpu.VMEM((8, BLK), jnp.int32), pltpu.SemaphoreType.DMA],
         flops=10**7,
         data=2 * 10**6,
-    )(own_map, oth_map, ords)
+        specs=[VM, VM, SM],
+    )(own_map, oth_map)
+    around = []
+    for k in range(nz):
+        around.append((k * 2, (k + 1) % nz * 2))
+        around.append(((k + 1) % nz * 2 + 1, k * 2 + 1))
     got = []
-    for d in range(1, nz // 2):
-        pairs = []
-        for k in range(nz):
-            pairs.append((((k + d) % nz) * 2, k * 2))
-            pairs.append((((k - d) % nz) * 2 + 1, k * 2 + 1))
-        got.append(lax.ppermute(comp, ("z", "co"), pairs))
-    got.append(lax.ppermute(part, "z", [((k + nz // 2) % nz, k) for k in range(nz)]))
-
+    held = comp
+    for _ in range(1, nz // 2 + 1):
+        held = lax.ppermute(held, ("z", "co"), around)
+        got.append(held)
+
+    weighted, anom_v, loc_v = call(
+        inner_kernel,
+        [shape((cells, half_cols), bf16), shape(anomalies.shape, bf16), shape(localization.shape, bf16)],
+        [HBM] * 4,
+        [pltpu.VMEM(innovations.shape, f32), pltpu.VMEM(obs_cell.shape, jnp.int32), pltpu.SemaphoreType.DMA((4,))],
+        flops=10**6,
+        data=4 * 10**6,
+    )(innovations, obs_cell, anomalies, localization)
     local, p_own = call(
         functools.partial(local_kernel, scale),
         [shape((cells, half_cols), bf16), shape((half_cols, half_cols), bf16)],
         [VM] * 5,
-        [pltpu.VMEM((cells + 2 * BLK, half_cols), bf16)],
         flops=10**9,
         data=4 * 10**6,
-    )(before, weighted, after, localization, anomalies)
+    )(before, weighted, after, loc_v, anom_v)
     far = lax.ppermute(near, "co", swap)
     (p_all,) = call(
         functools.partial(other_kernel, scale), [shape((half_cols, COLS), bf16)], [VM] * 4, flops=10**9, data=3 * 10**6
@@ -359,27 +397,29 @@
     )(f_own, f_oth, both, ords)
     recv = lax.all_to_all(msgs, "z", 0, 0, tiled=True)
 
-    near_maps = jnp.concatenate(got, axis=0)
-    near_maps, msgs = lax.optimization_barrier((near_maps, msgs))
-    far_maps = lax.ppermute(near_maps, "co", swap)
-    starts = [MSG * j + COLS for j in range(nz // 2 - 1)] + [MSG * (nz // 2 - 1) + COLS // 2]
-    tags = jnp.stack([jnp.stack([p[r, :NB] for r in starts]) for p in (near_maps, far_maps)]).astype(jnp.int32)
+    tied = lax.optimization_barrier((msgs, *got))
+    got = list(tied[1:])
+    for j in range(nz // 2 - 1):
+        got.append(lax.ppermute(got[j], "co", swap))
     maps, table = call(
         arrange_kernel,
-        [shape((nz, COLS, BLK), bf16), shape((nz, NB), jnp.int32)],
-        [VM, VM, SM],
+        [shape((nz, COLS, BLK), bf16), shape((nz, BLK), jnp.int32)],
+        [VM] * len(got),
+        [pltpu.VMEM((nz, BLK), jnp.int32), pltpu.SemaphoreType.DMA],
         flops=10**6,
         data=4 * 10**6,
         specs=[VM, SM],
-    )(near_maps, far_maps, tags)
+    )(*got)
     keep, send = call(
         sweep_kernel,
         [shape((2, hr, COLS), f32), shape((2, hr, COLS), bf16)],
-        [VM, VM, SM, VM, SM, VM, VM],
+        [VM, HBM, SM, VM, SM, VM, VM],
         [
+            pltpu.VMEM((nz, COLS, BLK), bf16),
             pltpu.VMEM((hr, COLS), f32),
             pltpu.VMEM((hr, COLS), f32),
             pltpu.VMEM((2, 2, hr, COLS), f32),
+            pltpu.SemaphoreType.DMA((nz,)),
         ],
         flops=10**9,
         data=3 * 10**6,

time: 109 us -> 100 us (0.917)
  waiting for transfers between devices: 52.6 us -> 40.5 us
  starting transfers between devices: 33.9 us -> 42.3 us
  local copies, waits for them, and re-layouts: 9.54 us -> 1.33 us
  Pallas kernels: 11.9 us -> 15.3 us
    all_to_all x1, waiting for transfers between devices: 15.2 us -> 0.01 us  [on_device(): recv = lax.all_to_all(msgs, 'z', 0, 0, tiled=True)]
    ppermute x5 -> x7, starting transfers between devices: 9.09 us -> 17.2 us  [the longest x4 12.9 us: on_device(): held = lax.ppermute(held, ('z', 'co'), around)]
    unnamed x20 -> x2, local copies, waits for them, and re-layouts: 8.37 us -> 1.33 us
    ppermute x5 -> x7, waiting for transfers between devices: 17.4 us -> 23.2 us  [the longest x4 21.8 us: on_device(): held = lax.ppermute(held, ('z', 'co'), around)]
    pallas_call x9 -> x10, Pallas kernels: 11.9 us -> 15.3 us  [run(): return made(*args)]
    all_to_all x1, starting transfers between devices: 5.83 us -> 8.17 us  [on_device(): recv = lax.all_to_all(msgs, 'z', 0, 0, tiled=True)]
    all_to_all x1, waiting for transfers between devices: 2.19 us -> 0.01 us  [on_device(): lax.all_to_all(p_all, 'lon', 0, 0, tiled=True).reshape(n_lon, rows, COLS)]
    ppermute x1, starting transfers between devices: 2.38 us -> 0.71 us  [on_device(): f_oth = lax.ppermute(f_send, 'co', swap)]
  transfers between devices with their start and end apart: 14 -> 16, of which waited for: 8 -> 12; matrix products, arithmetic and copies ran while one was open for 0% -> 0% of each run, Pallas kernels for 4% -> 7%
where the time goes in v1:
time: 100 us
  starting transfers between devices  42.3 us (42%)
  waiting for transfers between devices  40.5 us (40%)
  Pallas kernels  15.3 us (15%)
  local copies, waits for them, and re-layouts  1.33 us (1%)
    ppermute x4, waiting for transfers between devices, on_device(): held = lax.ppermute(held, ('z', 'co'), around)  21.8 us
    pallas_call x10, Pallas kernels, run(): return made(*args)  15.3 us
    ppermute x4, starting transfers between devices, on_device(): held = lax.ppermute(held, ('z', 'co'), around)  12.9 us
    ppermute x1, waiting for transfers between devices, on_device(): near = lax.ppermute(piece, 'ens', swap)  10.6 us
    all_to_all x1, starting transfers between devices, on_device(): recv = lax.all_to_all(msgs, 'z', 0, 0, tiled=True)  8.17 us
    all_to_all x1, starting transfers between devices, on_device(): lax.all_to_all(p_all, 'lon', 0, 0, tiled=True).reshape(n_lon, rows, COLS)  4.83 us
    ppermute x3, starting transfers between devices, on_device(): got.append(lax.ppermute(got[j], 'co', swap))  4.25 us
    ppermute x1, starting transfers between devices, on_device(): near = lax.ppermute(piece, 'ens', swap)  3.65 us
  transfers between devices with their start and end apart: 16, of which 12 were waited for; matrix products, arithmetic and copies ran while one was open for 0% of the time, Pallas kernels for 7%

profile of v1, /device:TPU:1, one launch (start us, length us, event | category | flops | bytes accessed | tf_op | source)
XLA Modules:
  0.0 100.1 jit_solution(9243976471318535310)
XLA Ops:
  0.6 1.4 %shard_map.77 = (bf16[128,512]{1,0:T(8,128)(2,1)S(1)}, bf16[128,512]{1,0:T(8,128)(2,1)S(1)}, bf16[512,512]{1,0:T(8,128)(2,1)S(1)}, bf16[1040,128]{1,0:T(8,128)(2,1)S(1)}) custom-call(f32[1,512]{1,0:T(1,128)} %innov.3, s32[1,512]{1,0:T(1,128)} %cell.3, bf16[1024,512]{1,0:T(8,128)(2,1)} %anom.3, f32[1024,128]{1,0:T(8,128)} %bitcast.2, s32[1,8]{1,0:T(1,128)} %order.1), custom_call_target="tpu_custom_call" | custom-call | flops 1000000 | bytes 2000000 | tf_op jit(solution)/shard_map/pallas_call | solution.py:38
  2.1 3.6 %collective-permute-start.2 = (bf16[512,512]{1,0:T(8,128)(2,1)S(1)}, bf16[512,512]{1,0:T(8,128)(2,1)S(1)}, u32[]{:S(2)}, u32[]{:S(2)}) collective-permute-start(bf16[512,512]{1,0:T(8,128)(2,1)S(1)} %get-tuple-element.30), channel_id=1, source_target_pairs={{0,1},{1,0},{2,3},{3,2},{4,5},{5,4},{6,7},{7,6},{8,9},{9,8},{10,11... | collective-permute-start | bytes 1572872 | tf_op jit(solution)/shard_map/ppermute | solution.py:339
  5.7 10.6 %collective-permute-done.2.near = bf16[512,512]{1,0:T(8,128)(2,1)S(1)} collective-permute-done((bf16[512,512]{1,0:T(8,128)(2,1)S(1)}, bf16[512,512]{1,0:T(8,128)(2,1)S(1)}, u32[]{:S(2)}, u32[]{:S(2)}) %collective-permute-start.2) | collective-permute-done | bytes 524320 | tf_op jit(solution)/shard_map/ppermute | solution.py:339
  16.3 2.3 %collective-permute-start.3 = (bf16[512,512]{1,0:T(8,128)(2,1)S(1)}, bf16[512,512]{1,0:T(8,128)(2,1)S(1)}, u32[]{:S(2)}, u32[]{:S(2)}) collective-permute-start(bf16[512,512]{1,0:T(8,128)(2,1)S(1)} %collective-permute-done.2.near), channel_id=1, source_target_pairs={{0,16},{16,0},{1,17},{17,1},{2,18},{18,2},{3,19},{19,3},{4,20},{20... | collective-permute-start | bytes 1572872 | tf_op jit(solution)/shard_map/ppermute | solution.py:378
  18.6 1.4 %collective-permute-start = (bf16[128,512]{1,0:T(8,128)(2,1)S(1)}, bf16[128,512]{1,0:T(8,128)(2,1)S(1)}, u32[]{:S(2)}, u32[]{:S(2)}) collective-permute-start(bf16[128,512]{1,0:T(8,128)(2,1)S(1)} %get-tuple-element.24), channel_id=1, source_target_pairs={{0,2},{2,4},{4,6},{6,8},{8,10},{10,12},{12,14},{14,0},{1,3},{3,5},... | collective-permute-start | bytes 393224 | tf_op jit(solution)/shard_map/ppermute | solution.py:340
  20.0 2.5 %collective-permute-start.1 = (bf16[128,512]{1,0:T(8,128)(2,1)S(1)}, bf16[128,512]{1,0:T(8,128)(2,1)S(1)}, u32[]{:S(2)}, u32[]{:S(2)}) collective-permute-start(bf16[128,512]{1,0:T(8,128)(2,1)S(1)} %get-tuple-element.26), channel_id=1, source_target_pairs={{2,0},{4,2},{6,4},{8,6},{10,8},{12,10},{14,12},{0,14},{3,1},{5,3},... | collective-permute-start | bytes 393224 | tf_op jit(solution)/shard_map/ppermute | solution.py:341
  22.5 1.5 %shard_map.78 = (bf16[1024,512]{1,0:T(8,128)(2,1)S(1)}, bf16[1024,512]{1,0:T(8,128)(2,1)S(1)}, bf16[8,3,128,128]{3,2,1,0:T(8,128)(2,1)S(1)}) custom-call(f32[1,512]{1,0:T(1,128)} %innov.3, s32[1,512]{1,0:T(1,128)} %cell.3, bf16[1024,512]{1,0:T(8,128)(2,1)} %anom.3, bf16[8,3,128,128]{3,2,1,0:T(8,128)(2,1)} %loc.1), custom_call_target="tpu_custom_call" | custom-call | flops 1000000 | bytes 4000000 | tf_op jit(solution)/shard_map/pallas_call | solution.py:38
  24.0 2.3 %collective-permute-done.before = bf16[128,512]{1,0:T(8,128)(2,1)S(1)} collective-permute-done((bf16[128,512]{1,0:T(8,128)(2,1)S(1)}, bf16[128,512]{1,0:T(8,128)(2,1)S(1)}, u32[]{:S(2)}, u32[]{:S(2)}) %collective-permute-start) | collective-permute-done | bytes 131104 | tf_op jit(solution)/shard_map/ppermute | solution.py:340
  26.3 1.3 %collective-permute-done.1.after = bf16[128,512]{1,0:T(8,128)(2,1)S(1)} collective-permute-done((bf16[128,512]{1,0:T(8,128)(2,1)S(1)}, bf16[128,512]{1,0:T(8,128)(2,1)S(1)}, u32[]{:S(2)}, u32[]{:S(2)}) %collective-permute-start.1) | collective-permute-done | bytes 131104 | tf_op jit(solution)/shard_map/ppermute | solution.py:341
  27.7 1.3 %shard_map.79 = (bf16[1024,512]{1,0:T(8,128)(2,1)S(1)}, bf16[512,512]{1,0:T(8,128)(2,1)S(1)}) custom-call(bf16[128,512]{1,0:T(8,128)(2,1)S(1)} %collective-permute-done.before, bf16[1024,512]{1,0:T(8,128)(2,1)S(1)} %get-tuple-element.25.mid, bf16[128,512]{1,0:T(8,128)(2,1)S(1)} %collective-permute-done.1.after, ...), custom_call_target="tpu_custom_call" | custom-call | flops 1000000000 | bytes 4000000 | tf_op jit(solution)/shard_map/pallas_call | solution.py:38
  29.0 0.0 collective-permute-done.3.far
  29.0 1.7 %shard_map.80 = bf16[512,1024]{1,0:T(8,128)(2,1)} custom-call(bf16[1024,512]{1,0:T(8,128)(2,1)S(1)} %get-tuple-element.29.lin, bf16[512,512]{1,0:T(8,128)(2,1)S(1)} %collective-permute-done.2.near, bf16[512,512]{1,0:T(8,128)(2,1)S(1)} %collective-permute-done.3.far, bf16[512,512]{1,0:T(8,128)(2,1)S(1)} %get-tuple-element.31.part), custom_call_target="tpu_custom_call" | custom-call | flops 1000000000 | bytes 3000000 | tf_op jit(solution)/shard_map/pallas_call | solution.py:38
  30.7 4.8 %all-to-all-start = ((bf16[8,64,1024]{2,1,0:T(8,128)(2,1)}), bf16[8,64,1024]{2,1,0:T(8,128)(2,1)S(1)}, u32[]{:S(2)}, u32[]{:S(2)}) async-start(bf16[8,64,1024]{2,1,0:T(8,128)(2,1)} %bitcast.1), calls=%async_computation | async-start | bytes 2097152 | tf_op jit(solution)/shard_map/all_to_all | solution.py:383
  35.5 1.1 %collective-permute-start.5 = (bf16[1040,128]{1,0:T(8,128)(2,1)S(1)}, bf16[1040,128]{1,0:T(8,128)(2,1)S(1)}, u32[]{:S(2)}, u32[]{:S(2)}) collective-permute-start(bf16[1040,128]{1,0:T(8,128)(2,1)S(1)} %get-tuple-element.34.own), channel_id=1, source_target_pairs={{0,16},{16,0},{1,17},{17,1},{2,18},{18,2},{3,19},{19,3},{4,20},{20... | collective-permute-start | bytes 798728 | tf_op jit(solution)/shard_map/ppermute | solution.py:342
  36.7 1.2 %collective-permute-done.5.oth = bf16[1040,128]{1,0:T(8,128)(2,1)S(1)} collective-permute-done((bf16[1040,128]{1,0:T(8,128)(2,1)S(1)}, bf16[1040,128]{1,0:T(8,128)(2,1)S(1)}, u32[]{:S(2)}, u32[]{:S(2)}) %collective-permute-start.5) | collective-permute-done | bytes 266272 | tf_op jit(solution)/shard_map/ppermute | solution.py:342
  37.8 1.3 %shard_map.82 = (bf16[2,1024,128]{2,1,0:T(8,128)(2,1)S(1)}, bf16[1040,128]{1,0:T(8,128)(2,1)S(1)}, s32[8,128]{1,0:T(8,128)S(1)}) custom-call(bf16[1040,128]{1,0:T(8,128)(2,1)S(1)} %get-tuple-element.34.own, bf16[1040,128]{1,0:T(8,128)(2,1)S(1)} %collective-permute-done.5.oth), custom_call_target="tpu_custom_call" | custom-call | flops 10000000 | bytes 2000000 | tf_op jit(solution)/shard_map/pallas_call | solution.py:38
  39.2 5.6 %collective-permute-start.6 = (bf16[1040,128]{1,0:T(8,128)(2,1)S(1)}, bf16[1040,128]{1,0:T(8,128)(2,1)S(1)}, u32[]{:S(2)}, u32[]{:S(2)}) collective-permute-start(bf16[1040,128]{1,0:T(8,128)(2,1)S(1)} %get-tuple-element.37), channel_id=1, source_target_pairs={{0,32},{48,16},{32,64},{80,48},{64,96},{112,80},{96,128},{144,112}... | collective-permute-start | bytes 798728 | tf_op jit(solution)/shard_map/ppermute | solution.py:360
  44.8 3.4 %collective-permute-done.6.refs_0_ = bf16[1040,128]{1,0:T(8,128)(2,1)S(1)} collective-permute-done((bf16[1040,128]{1,0:T(8,128)(2,1)S(1)}, bf16[1040,128]{1,0:T(8,128)(2,1)S(1)}, u32[]{:S(2)}, u32[]{:S(2)}) %collective-permute-start.6) | collective-permute-done | bytes 266272 | tf_op jit(solution)/shard_map/ppermute | solution.py:360
  48.2 3.4 %collective-permute-start.7 = (bf16[1040,128]{1,0:T(8,128)(2,1)S(1)}, bf16[1040,128]{1,0:T(8,128)(2,1)S(1)}, u32[]{:S(2)}, u32[]{:S(2)}) collective-permute-start(bf16[1040,128]{1,0:T(8,128)(2,1)S(1)} %collective-permute-done.6.refs_0_), channel_id=1, source_target_pairs={{0,32},{48,16},{32,64},{80,48},{64,96},{112,80},{96,128},{144,112}... | collective-permute-start | bytes 798728 | tf_op jit(solution)/shard_map/ppermute | solution.py:360
  51.6 0.0 all-to-all-done.parts
  51.6 0.1 shard_map.81
  51.7 0.7 collective-permute-start.4
  52.4 0.9 collective-permute-done.4.oth
  53.3 1.9 %shard_map.83 = bf16[8,32,1024]{2,1,0:T(8,128)(2,1)} custom-call(f32[32,1024]{1,0:T(8,128)S(1)} %get-tuple-element.32.own, bf16[32,1024]{1,0:T(8,128)(2,1)S(1)} %collective-permute-done.4.oth, bf16[2,1024,128]{2,1,0:T(8,128)(2,1)S(1)} %get-tuple-element.35.both, s32[8,128]{1,0:T(8,128)S(1)} %get-tuple-element.36.ords), custom_call_target="tpu_custom_call" | custom-call | flops 100000000 | bytes 1000000 | tf_op jit(solution)/shard_map/pallas_call | solution.py:38
  55.2 8.2 %all-to-all-start.1 = ((bf16[8,32,1024]{2,1,0:T(8,128)(2,1)}), bf16[8,32,1024]{2,1,0:T(8,128)(2,1)S(1)}, u32[]{:S(2)}, u32[]{:S(2)}) async-start(bf16[8,32,1024]{2,1,0:T(8,128)(2,1)} %shard_map.83), calls=%async_computation.1 | async-start | bytes 1048576 | tf_op jit(solution)/shard_map/all_to_all | solution.py:398
  63.4 0.0 collective-permute-done.7.refs_1_
  63.4 2.7 %collective-permute-start.8 = (bf16[1040,128]{1,0:T(8,128)(2,1)S(1)}, bf16[1040,128]{1,0:T(8,128)(2,1)S(1)}, u32[]{:S(2)}, u32[]{:S(2)}) collective-permute-start(bf16[1040,128]{1,0:T(8,128)(2,1)S(1)} %collective-permute-done.7.refs_1_), channel_id=1, source_target_pairs={{0,32},{48,16},{32,64},{80,48},{64,96},{112,80},{96,128},{144,112}... | collective-permute-start | bytes 798728 | tf_op jit(solution)/shard_map/ppermute | solution.py:360
  66.1 14.3 %collective-permute-done.8.refs_2_ = bf16[1040,128]{1,0:T(8,128)(2,1)S(1)} collective-permute-done((bf16[1040,128]{1,0:T(8,128)(2,1)S(1)}, bf16[1040,128]{1,0:T(8,128)(2,1)S(1)}, u32[]{:S(2)}, u32[]{:S(2)}) %collective-permute-start.8) | collective-permute-done | bytes 266272 | tf_op jit(solution)/shard_map/ppermute | solution.py:360
  80.4 1.2 %collective-permute-start.9 = (bf16[1040,128]{1,0:T(8,128)(2,1)S(1)}, bf16[1040,128]{1,0:T(8,128)(2,1)S(1)}, u32[]{:S(2)}, u32[]{:S(2)}) collective-permute-start(bf16[1040,128]{1,0:T(8,128)(2,1)S(1)} %collective-permute-done.8.refs_2_), channel_id=1, source_target_pairs={{0,32},{48,16},{32,64},{80,48},{64,96},{112,80},{96,128},{144,112}... | collective-permute-start | bytes 798728 | tf_op jit(solution)/shard_map/ppermute | solution.py:360
  81.6 4.1 %collective-permute-done.9.refs_3_ = bf16[1040,128]{1,0:T(8,128)(2,1)S(1)} collective-permute-done((bf16[1040,128]{1,0:T(8,128)(2,1)S(1)}, bf16[1040,128]{1,0:T(8,128)(2,1)S(1)}, u32[]{:S(2)}, u32[]{:S(2)}) %collective-permute-start.9) | collective-permute-done | bytes 266272 | tf_op jit(solution)/shard_map/ppermute | solution.py:360
  85.7 3.7 %collective-permute-start.10 = (bf16[1040,128]{1,0:T(8,128)(2,1)S(1)}, bf16[1040,128]{1,0:T(8,128)(2,1)S(1)}, u32[]{:S(2)}, u32[]{:S(2)}) collective-permute-start(bf16[1040,128]{1,0:T(8,128)(2,1)S(1)} %collective-permute-done.6.refs_0_), channel_id=1, source_target_pairs={{0,16},{16,0},{1,17},{17,1},{2,18},{18,2},{3,19},{19,3},{4,20},{20... | collective-permute-start | bytes 798728 | tf_op jit(solution)/shard_map/ppermute | solution.py:403
  89.4 0.0 collective-permute-start.11
  89.4 0.5 collective-permute-start.12
  89.9 0.7 collective-permute-done.10.refs_4_
  90.6 0.4 collective-permute-done.11.refs_5_
  90.9 0.4 collective-permute-done.12.refs_6_
  91.3 1.4 %shard_map.84 = (bf16[8,1024,128]{2,1,0:T(8,128)(2,1)S(1)}, s32[8,128]{1,0:T(8,128)S(1)}) custom-call(bf16[1040,128]{1,0:T(8,128)(2,1)S(1)} %collective-permute-done.6.refs_0_, bf16[1040,128]{1,0:T(8,128)(2,1)S(1)} %collective-permute-done.7.refs_1_, bf16[1040,128]{1,0:T(8,128)(2,1)S(1)} %collective-permute-done.8.refs_2_, ...), custom_call_target="tpu_custom_call" | custom-call | flops 1000000 | bytes 4000000 | tf_op jit(solution)/shard_map/pallas_call | solution.py:38
  92.7 0.0 copy-start
  92.7 1.3 %copy-done = bf16[8,1024,128]{2,1,0:T(8,128)(2,1)} copy-done((bf16[8,1024,128]{2,1,0:T(8,128)(2,1)}, bf16[8,1024,128]{2,1,0:T(8,128)(2,1)S(1)}, u32[]{:S(2)}) %copy-start) | copy-done | bytes 2097176
  94.0 0.0 all-to-all-done.1.recv
  94.0 3.8 %shard_map.85 = (f32[2,32,1024]{2,1,0:T(8,128)S(1)}, bf16[2,32,1024]{2,1,0:T(8,128)(2,1)S(1)}) custom-call(bf16[8,32,1024]{2,1,0:T(8,128)(2,1)S(1)} %all-to-all-done.1.recv, bf16[8,1024,128]{2,1,0:T(8,128)(2,1)} %copy-done, s32[8,128]{1,0:T(8,128)S(1)} %get-tuple-element.43.tags, bf16[2,1024,128]{2,1,0:T(8,128)(2,1)S(1)} %get-tuple-element.35.both, ...), custom_call_target="tpu_custom_call" | custom-call | flops 1000000000 | bytes 3000000 | tf_op jit(solution)/shard_map/pallas_call | solution.py:38
  97.8 0.5 collective-permute-start.13
  98.3 1.0 collective-permute-done.13.back
  99.3 0.8 shard_map.86
Async XLA Ops:
  2.1 14.3 %collective-permute-start.2 = (bf16[512,512]{1,0:T(8,128)(2,1)S(1)}, bf16[512,512]{1,0:T(8,128)(2,1)S(1)}, u32[]{:S(2)}, u32[]{:S(2)}) collective-permute-start(bf16[512,512]{1,0:T(8,128)(2,1)S(1)} %get-tuple-element.30), channel_id=1, source_target_pairs={{0,1},{1,0},{2,3},{3,2},{4,5},{5,4},{6,7},{7,6},{8,9},{9,8},{10,11... | collective-permute-start | bytes 1572872 | tf_op jit(solution)/shard_map/ppermute | solution.py:339
  16.3 12.6 %collective-permute-start.3 = (bf16[512,512]{1,0:T(8,128)(2,1)S(1)}, bf16[512,512]{1,0:T(8,128)(2,1)S(1)}, u32[]{:S(2)}, u32[]{:S(2)}) collective-permute-start(bf16[512,512]{1,0:T(8,128)(2,1)S(1)} %collective-permute-done.2.near), channel_id=1, source_target_pairs={{0,16},{16,0},{1,17},{17,1},{2,18},{18,2},{3,19},{19,3},{4,20},{20... | collective-permute-start | bytes 1572872 | tf_op jit(solution)/shard_map/ppermute | solution.py:378
  18.6 7.8 %collective-permute-start = (bf16[128,512]{1,0:T(8,128)(2,1)S(1)}, bf16[128,512]{1,0:T(8,128)(2,1)S(1)}, u32[]{:S(2)}, u32[]{:S(2)}) collective-permute-start(bf16[128,512]{1,0:T(8,128)(2,1)S(1)} %get-tuple-element.24), channel_id=1, source_target_pairs={{0,2},{2,4},{4,6},{6,8},{8,10},{10,12},{12,14},{14,0},{1,3},{3,5},... | collective-permute-start | bytes 393224 | tf_op jit(solution)/shard_map/ppermute | solution.py:340
  20.0 7.7 %collective-permute-start.1 = (bf16[128,512]{1,0:T(8,128)(2,1)S(1)}, bf16[128,512]{1,0:T(8,128)(2,1)S(1)}, u32[]{:S(2)}, u32[]{:S(2)}) collective-permute-start(bf16[128,512]{1,0:T(8,128)(2,1)S(1)} %get-tuple-element.26), channel_id=1, source_target_pairs={{2,0},{4,2},{6,4},{8,6},{10,8},{12,10},{14,12},{0,14},{3,1},{5,3},... | collective-permute-start | bytes 393224 | tf_op jit(solution)/shard_map/ppermute | solution.py:341
  30.7 20.9 %all-to-all-start = ((bf16[8,64,1024]{2,1,0:T(8,128)(2,1)}), bf16[8,64,1024]{2,1,0:T(8,128)(2,1)S(1)}, u32[]{:S(2)}, u32[]{:S(2)}) async-start(bf16[8,64,1024]{2,1,0:T(8,128)(2,1)} %bitcast.1), calls=%async_computation | async-start | bytes 2097152 | tf_op jit(solution)/shard_map/all_to_all | solution.py:383
  35.5 2.3 %collective-permute-start.5 = (bf16[1040,128]{1,0:T(8,128)(2,1)S(1)}, bf16[1040,128]{1,0:T(8,128)(2,1)S(1)}, u32[]{:S(2)}, u32[]{:S(2)}) collective-permute-start(bf16[1040,128]{1,0:T(8,128)(2,1)S(1)} %get-tuple-element.34.own), channel_id=1, source_target_pairs={{0,16},{16,0},{1,17},{17,1},{2,18},{18,2},{3,19},{19,3},{4,20},{20... | collective-permute-start | bytes 798728 | tf_op jit(solution)/shard_map/ppermute | solution.py:342
  39.2 9.0 %collective-permute-start.6 = (bf16[1040,128]{1,0:T(8,128)(2,1)S(1)}, bf16[1040,128]{1,0:T(8,128)(2,1)S(1)}, u32[]{:S(2)}, u32[]{:S(2)}) collective-permute-start(bf16[1040,128]{1,0:T(8,128)(2,1)S(1)} %get-tuple-element.37), channel_id=1, source_target_pairs={{0,32},{48,16},{32,64},{80,48},{64,96},{112,80},{96,128},{144,112}... | collective-permute-start | bytes 798728 | tf_op jit(solution)/shard_map/ppermute | solution.py:360
  48.2 15.2 %collective-permute-start.7 = (bf16[1040,128]{1,0:T(8,128)(2,1)S(1)}, bf16[1040,128]{1,0:T(8,128)(2,1)S(1)}, u32[]{:S(2)}, u32[]{:S(2)}) collective-permute-start(bf16[1040,128]{1,0:T(8,128)(2,1)S(1)} %collective-permute-done.6.refs_0_), channel_id=1, source_target_pairs={{0,32},{48,16},{32,64},{80,48},{64,96},{112,80},{96,128},{144,112}... | collective-permute-start | bytes 798728 | tf_op jit(solution)/shard_map/ppermute | solution.py:360
  51.7 1.6 %collective-permute-start.4 = (bf16[32,1024]{1,0:T(8,128)(2,1)S(1)}, bf16[32,1024]{1,0:T(8,128)(2,1)S(1)}, u32[]{:S(2)}, u32[]{:S(2)}) collective-permute-start(bf16[32,1024]{1,0:T(8,128)(2,1)S(1)} %get-tuple-element.33), channel_id=1, source_target_pairs={{0,16},{16,0},{1,17},{17,1},{2,18},{18,2},{3,19},{19,3},{4,20},{20... | collective-permute-start | bytes 196616 | tf_op jit(solution)/shard_map/ppermute | solution.py:389
  55.2 38.8 %all-to-all-start.1 = ((bf16[8,32,1024]{2,1,0:T(8,128)(2,1)}), bf16[8,32,1024]{2,1,0:T(8,128)(2,1)S(1)}, u32[]{:S(2)}, u32[]{:S(2)}) async-start(bf16[8,32,1024]{2,1,0:T(8,128)(2,1)} %shard_map.83), calls=%async_computation.1 | async-start | bytes 1048576 | tf_op jit(solution)/shard_map/all_to_all | solution.py:398
  63.4 17.0 %collective-permute-start.8 = (bf16[1040,128]{1,0:T(8,128)(2,1)S(1)}, bf16[1040,128]{1,0:T(8,128)(2,1)S(1)}, u32[]{:S(2)}, u32[]{:S(2)}) collective-permute-start(bf16[1040,128]{1,0:T(8,128)(2,1)S(1)} %collective-permute-done.7.refs_1_), channel_id=1, source_target_pairs={{0,32},{48,16},{32,64},{80,48},{64,96},{112,80},{96,128},{144,112}... | collective-permute-start | bytes 798728 | tf_op jit(solution)/shard_map/ppermute | solution.py:360
  80.4 5.3 %collective-permute-start.9 = (bf16[1040,128]{1,0:T(8,128)(2,1)S(1)}, bf16[1040,128]{1,0:T(8,128)(2,1)S(1)}, u32[]{:S(2)}, u32[]{:S(2)}) collective-permute-start(bf16[1040,128]{1,0:T(8,128)(2,1)S(1)} %collective-permute-done.8.refs_2_), channel_id=1, source_target_pairs={{0,32},{48,16},{32,64},{80,48},{64,96},{112,80},{96,128},{144,112}... | collective-permute-start | bytes 798728 | tf_op jit(solution)/shard_map/ppermute | solution.py:360
  85.7 4.9 %collective-permute-start.10 = (bf16[1040,128]{1,0:T(8,128)(2,1)S(1)}, bf16[1040,128]{1,0:T(8,128)(2,1)S(1)}, u32[]{:S(2)}, u32[]{:S(2)}) collective-permute-start(bf16[1040,128]{1,0:T(8,128)(2,1)S(1)} %collective-permute-done.6.refs_0_), channel_id=1, source_target_pairs={{0,16},{16,0},{1,17},{17,1},{2,18},{18,2},{3,19},{19,3},{4,20},{20... | collective-permute-start | bytes 798728 | tf_op jit(solution)/shard_map/ppermute | solution.py:403
  89.4 1.5 %collective-permute-start.11 = (bf16[1040,128]{1,0:T(8,128)(2,1)S(1)}, bf16[1040,128]{1,0:T(8,128)(2,1)S(1)}, u32[]{:S(2)}, u32[]{:S(2)}) collective-permute-start(bf16[1040,128]{1,0:T(8,128)(2,1)S(1)} %collective-permute-done.7.refs_1_), channel_id=1, source_target_pairs={{0,16},{16,0},{1,17},{17,1},{2,18},{18,2},{3,19},{19,3},{4,20},{20... | collective-permute-start | bytes 798728 | tf_op jit(solution)/shard_map/ppermute | solution.py:403
  89.4 1.9 %collective-permute-start.12 = (bf16[1040,128]{1,0:T(8,128)(2,1)S(1)}, bf16[1040,128]{1,0:T(8,128)(2,1)S(1)}, u32[]{:S(2)}, u32[]{:S(2)}) collective-permute-start(bf16[1040,128]{1,0:T(8,128)(2,1)S(1)} %collective-permute-done.8.refs_2_), channel_id=1, source_target_pairs={{0,16},{16,0},{1,17},{17,1},{2,18},{18,2},{3,19},{19,3},{4,20},{20... | collective-permute-start | bytes 798728 | tf_op jit(solution)/shard_map/ppermute | solution.py:403
  92.7 1.3 %copy-start = (bf16[8,1024,128]{2,1,0:T(8,128)(2,1)}, bf16[8,1024,128]{2,1,0:T(8,128)(2,1)S(1)}, u32[]{:S(2)}) copy-start(bf16[8,1024,128]{2,1,0:T(8,128)(2,1)S(1)} %get-tuple-element.42.stored) | copy-start | bytes 6291460
  97.8 1.4 %collective-permute-start.13 = (bf16[2,32,1024]{2,1,0:T(8,128)(2,1)S(1)}, bf16[2,32,1024]{2,1,0:T(8,128)(2,1)S(1)}, u32[]{:S(2)}, u32[]{:S(2)}) collective-permute-start(bf16[2,32,1024]{2,1,0:T(8,128)(2,1)S(1)} %get-tuple-element.45), channel_id=1, source_target_pairs={{0,16},{16,0},{1,17},{17,1},{2,18},{18,2},{3,19},{19,3},{4,20},{20... | collective-permute-start | bytes 393224 | tf_op jit(solution)/shard_map/ppermute | solution.py:427

commit v2 on v1

--- a/solution.py
+++ b/solution.py
@@ -55,17 +55,14 @@
     return jnp.sum(jnp.where(ids == cell[...], innov[...], 0.0), axis=1, keepdims=True)
 
 
-def entry_kernel(innov, cell, anom, tang, order, head, tail, piece, msg, innov_v, cell_v, edge, tang_v, order_s, sem):
-    co = lax.axis_index("co")
+def entry_kernel(innov, cell, anom, tang, order, head, tail, msg, innov_v, cell_v, edge, tang_v, order_s, sem):
     cells = anom.shape[0]
-    h = piece.shape[0]
     pairs = (
         (innov, innov_v),
         (cell, cell_v),
         (anom.at[pl.ds(0, BLK)], edge.at[0]),
         (anom.at[pl.ds(cells - BLK, BLK)], edge.at[1]),
         (tang, tang_v),
-        (anom.at[pl.ds(pl.multiple_of(co * h, h), h)], piece),
         (order, order_s),
     )
     copies = [pltpu.make_async_copy(a, b, sem.at[i]) for i, (a, b) in enumerate(pairs)]
@@ -79,7 +76,7 @@
     copies[3].wait()
     head[...] = (w0 * edge[0].astype(f32)).astype(bf16)
     tail[...] = (w1 * edge[1].astype(f32)).astype(bf16)
-    copies[6].wait()
+    copies[5].wait()
     lane = lax.broadcasted_iota(jnp.int32, (16, BLK), 1)
     tag = jnp.zeros((16, BLK), f32)
     for i in range(NB):
@@ -87,7 +84,6 @@
     msg[COLS:] = tag.astype(bf16)
     copies[4].wait()
     msg[:COLS] = tang_v[...].astype(bf16)
-    copies[5].wait()
 
 
 def inner_kernel(innov, cell, anom, loc, out, anom_v, loc_v, innov_v, cell_v, sem):
@@ -106,7 +102,7 @@
     copies[3].wait()
 
 
-def local_kernel(scale, before, mid, after, loc, anom, lout, pout):
+def local_kernel(before, mid, after, loc, lout):
     n = mid.shape[0] // BLK
     for b in range(n):
         left = jnp.concatenate([loc[b, 0], loc[b, 1], loc[b, 2]], axis=1)
@@ -118,22 +114,27 @@
             right = mid[(b - 1) * BLK : (b + 2) * BLK]
         y = jnp.dot(left, right, preferred_element_type=f32)
         lout[b * BLK : (b + 1) * BLK] = y.astype(bf16)
-    y = lax.dot_general(lout[...], anom[...], (((0,), (0,)), ((), ())), preferred_element_type=f32)
-    pout[...] = (y * scale).astype(bf16)
-
-
-def other_kernel(scale, lin, near, far, part, pout):
-    co = lax.axis_index("co")
-    e = lax.axis_index("ens")
-    n = near.shape[0]
-    half = part.shape[1]
+
+
+def product_kernel(scale, mine, theirs, anom, fetched, pout):
+    co = lax.axis_index("co")
+    half = anom.shape[1]
     dims = (((0,), (0,)), ((), ()))
-    mine = lin[pl.ds(pl.multiple_of(co * n, n), n), :]
-    rest = lin[pl.ds(pl.multiple_of((1 - co) * n, n), n), :]
-    y = lax.dot_general(mine, near[...], dims, preferred_element_type=f32)
-    y = y + lax.dot_general(rest, far[...], dims, preferred_element_type=f32)
-    pout[:, pl.ds(pl.multiple_of(e * half, half), half)] = part[...]
-    pout[:, pl.ds(pl.multiple_of((1 - e) * half, half), half)] = (y * scale).astype(bf16)
+
+    def fill(right):
+        for src, t in ((mine, co), (theirs, 1 - co)):
+            y = lax.dot_general(src[...], right[...], dims, preferred_element_type=f32)
+            pout[:, pl.ds(pl.multiple_of(t * half, half), half)] = (y * scale).astype(bf16)
+
+    own = co == lax.axis_index("ens")
+
+    @pl.when(own)
+    def _():
+        fill(anom)
+
+    @pl.when(jnp.logical_not(own))
+    def _():
+        fill(fetched)
 
 
 def map_kernel(own, oth, both, comp, ords, ints, sem):
@@ -214,14 +215,20 @@
     return lambda i: both[t, i * BLK : (i + 1) * BLK]
 
 
-def total_kernel(own, oth, both, ords, out, low, tot, tmp):
-    co = lax.axis_index("co")
+def assemble(force, own, oth):
+    co = lax.axis_index("co")
+    half = COLS // 2
+    for src, place in ((own, co), (oth, 1 - co)):
+        at = pl.ds(pl.multiple_of(place * half, half), half)
+        for t in range(2):
+            force[t, :, at] = src[:, t * half : (t + 1) * half].astype(f32)
+    return force[0], force[1]
+
+
+def total_kernel(own, oth, both, ords, out, force, tot, tmp):
     z = lax.axis_index("z")
-    mine = own[...]
-    other = oth[...].astype(f32)
-    first = jnp.where(co == 0, mine, other)
-    second = jnp.where(co == 0, other, mine)
-    low[...] = first
+    first, second = assemble(force, own, oth)
+    low = force.at[0]
     ys = apply_adjoint([cut(second, i) for i in range(NB)], block_of(both, 1))
     fs = apply_forward(low, block_of(both, 1), lambda i: ords[1, i], lambda i: cut(second, i))
     for i in range(NB):
@@ -236,7 +243,7 @@
         out[d] = jnp.where(d > z, fwd, adj)
 
 
-def sweep_kernel(recv, stored, tags, both, ords, own, oth, keep, send, maps, st, adj, res, sem):
+def sweep_kernel(recv, stored, tags, both, ords, own, oth, keep, send, maps, st, adj, res, split_force, sem):
     co = lax.axis_index("co")
     z = lax.axis_index("z")
     nz = recv.shape[0]
@@ -251,9 +258,7 @@
             def _():
                 copy(k).start()
 
-    mine = own[...]
-    other = oth[...].astype(f32)
-    force = (jnp.where(co == 0, mine, other), jnp.where(co == 0, other, mine))
+    force = assemble(split_force, own, oth)
     st[...] = jnp.where(z > 0, recv[0].astype(f32), 0.0)
     adj[...] = jnp.where(z < nz - 1, recv[nz - 1].astype(f32), 0.0)
 
@@ -314,12 +319,11 @@
     swap = [(0, 1), (1, 0)]
     scale = float(cells * n_lon) ** (-0.5)
 
-    head, tail, piece, own_map = call(
+    head, tail, own_map = call(
         entry_kernel,
         [
             shape((BLK, half_cols), bf16),
             shape((BLK, half_cols), bf16),
-            shape((cells // 2, half_cols), bf16),
             shape((MSG, BLK), bf16),
         ],
         [HBM] * 5,
@@ -329,14 +333,14 @@
             pltpu.VMEM((2, BLK, half_cols), bf16),
             pltpu.VMEM((COLS, BLK), f32),
             pltpu.SMEM(tangent_order.shape, jnp.int32),
-            pltpu.SemaphoreType.DMA((7,)),
+            pltpu.SemaphoreType.DMA((6,)),
         ],
         flops=10**6,
         data=2 * 10**6,
     )(innovations, obs_cell, anomalies, tangent_blocks.reshape(COLS, BLK), tangent_order)
     up = [(i, (i + 1) % n_lon) for i in range(n_lon)]
     down = [(b, a) for a, b in up]
-    near = lax.ppermute(piece, "ens", swap)
+    fetched = lax.ppermute(anomalies, ("co", "ens"), [(0, 1), (3, 2)])
     before = lax.ppermute(tail, "lon", up)
     after = lax.ppermute(head, "lon", down)
     oth_map = lax.ppermute(own_map, "co", swap)
@@ -368,17 +372,13 @@
         flops=10**6,
         data=4 * 10**6,
     )(innovations, obs_cell, anomalies, localization)
-    local, p_own = call(
-        functools.partial(local_kernel, scale),
-        [shape((cells, half_cols), bf16), shape((half_cols, half_cols), bf16)],
-        [VM] * 5,
-        flops=10**9,
-        data=4 * 10**6,
-    )(before, weighted, after, loc_v, anom_v)
-    far = lax.ppermute(near, "co", swap)
+    (local,) = call(local_kernel, [shape((cells, half_cols), bf16)], [VM] * 4, flops=10**9, data=4 * 10**6)(
+        before, weighted, after, loc_v
+    )
+    local_oth = lax.ppermute(local, "co", swap)
     (p_all,) = call(
-        functools.partial(other_kernel, scale), [shape((half_cols, COLS), bf16)], [VM] * 4, flops=10**9, data=3 * 10**6
-    )(local, near, far, p_own)
+        functools.partial(product_kernel, scale), [shape((half_cols, COLS), bf16)], [VM] * 4, flops=10**9, data=3 * 10**6
+    )(local, local_oth, anom_v, fetched)
     rows = half_cols // n_lon
     parts = lax.all_to_all(p_all, "lon", 0, 0, tiled=True).reshape(n_lon, rows, COLS)
 
@@ -391,7 +391,7 @@
         total_kernel,
         [shape((nz, hr, COLS), bf16)],
         [VM, VM, VM, SM],
-        [pltpu.VMEM((hr, COLS), f32), pltpu.VMEM((hr, COLS), bf16), pltpu.VMEM((hr, COLS), f32)],
+        [pltpu.VMEM((2, hr, COLS), f32), pltpu.VMEM((hr, COLS), bf16), pltpu.VMEM((hr, COLS), f32)],
         flops=10**8,
         data=10**6,
     )(f_own, f_oth, both, ords)
@@ -419,6 +419,7 @@
             pltpu.VMEM((hr, COLS), f32),
             pltpu.VMEM((hr, COLS), f32),
             pltpu.VMEM((2, 2, hr, COLS), f32),
+            pltpu.VMEM((2, hr, COLS), f32),
             pltpu.SemaphoreType.DMA((nz,)),
         ],
         flops=10**9,

time: 100 us -> 96.1 us (0.961)
  waiting for transfers between devices: 40.5 us -> 38.3 us
  starting transfers between devices: 42.3 us -> 40.3 us
    ppermute x1, waiting for transfers between devices: 2.34 us -> 0.01 us  [on_device(): before = lax.ppermute(tail, 'lon', up)]
    ppermute x2, starting transfers between devices: 5.92 us -> 4.52 us  [the longest x1 3.24 us: on_device(): local_oth = lax.ppermute(local, 'co', swap)]
    ppermute x2, waiting for transfers between devices: 10.6 us -> 9.3 us  [the longest x1 9.3 us: on_device(): fetched = lax.ppermute(anomalies, ('co', 'ens'), [(0, 1), (3, 2)])]
    ppermute x1, starting transfers between devices: 1.13 us -> 0.01 us  [on_device(): oth_map = lax.ppermute(own_map, 'co', swap)]
where the time goes in v2:
time: 96.1 us; the launch traced here: 95.8 us
  starting transfers between devices  40.3 us (42%)
  waiting for transfers between devices  38.3 us (40%)
  Pallas kernels  15.1 us (16%)
  local copies, waits for them, and re-layouts  1.33 us (1%)
    ppermute x4, waiting for transfers between devices, on_device(): held = lax.ppermute(held, ('z', 'co'), around)  21.8 us
    pallas_call x10, Pallas kernels, run(): return made(*args)  15.1 us
    ppermute x4, starting transfers between devices, on_device(): held = lax.ppermute(held, ('z', 'co'), around)  12.9 us
    ppermute x1, waiting for transfers between devices, on_device(): fetched = lax.ppermute(anomalies, ('co', 'ens'), [(0, 1), (3, 2)])  9.3 us
    all_to_all x1, starting transfers between devices, on_device(): recv = lax.all_to_all(msgs, 'z', 0, 0, tiled=True)  8.18 us
    all_to_all x1, starting transfers between devices, on_device(): lax.all_to_all(p_all, 'lon', 0, 0, tiled=True).reshape(n_lon, rows, COLS)  4.56 us
    ppermute x3, starting transfers between devices, on_device(): got.append(lax.ppermute(got[j], 'co', swap))  4.25 us
    ppermute x1, starting transfers between devices, on_device(): local_oth = lax.ppermute(local, 'co', swap)  3.24 us
  transfers between devices with their start and end apart: 16, of which 12 were waited for; matrix products, arithmetic and copies ran while one was open for 0% of the time, Pallas kernels for 7%

profile of v2, /device:TPU:1, one launch (start us, length us, event | category | flops | bytes accessed | tf_op | source)
XLA Modules:
  0.0 95.8 jit_solution(17135407683717131000)
XLA Ops:
  0.6 1.3 %shard_map.77 = (bf16[128,512]{1,0:T(8,128)(2,1)S(1)}, bf16[128,512]{1,0:T(8,128)(2,1)S(1)}, bf16[1040,128]{1,0:T(8,128)(2,1)S(1)}) custom-call(f32[1,512]{1,0:T(1,128)} %innov.3, s32[1,512]{1,0:T(1,128)} %cell.3, bf16[1024,512]{1,0:T(8,128)(2,1)} %anom.3, f32[1024,128]{1,0:T(8,128)} %bitcast.2, s32[1,8]{1,0:T(1,128)} %order.1), custom_call_target="tpu_custom_call" | custom-call | flops 1000000 | bytes 2000000 | tf_op jit(solution)/shard_map/pallas_call | solution.py:38
  1.9 2.1 %collective-permute-start = (bf16[128,512]{1,0:T(8,128)(2,1)S(1)}, bf16[128,512]{1,0:T(8,128)(2,1)S(1)}, u32[]{:S(2)}, u32[]{:S(2)}) collective-permute-start(bf16[128,512]{1,0:T(8,128)(2,1)S(1)} %get-tuple-element.21), channel_id=1, source_target_pairs={{0,2},{2,4},{4,6},{6,8},{8,10},{10,12},{12,14},{14,0},{1,3},{3,5},... | collective-permute-start | bytes 393224 | tf_op jit(solution)/shard_map/ppermute | solution.py:344
  4.0 2.5 %collective-permute-start.1 = (bf16[128,512]{1,0:T(8,128)(2,1)S(1)}, bf16[128,512]{1,0:T(8,128)(2,1)S(1)}, u32[]{:S(2)}, u32[]{:S(2)}) collective-permute-start(bf16[128,512]{1,0:T(8,128)(2,1)S(1)} %get-tuple-element.23), channel_id=1, source_target_pairs={{2,0},{4,2},{6,4},{8,6},{10,8},{12,10},{14,12},{0,14},{3,1},{5,3},... | collective-permute-start | bytes 393224 | tf_op jit(solution)/shard_map/ppermute | solution.py:345
  6.6 1.3 %collective-permute-start.3 = (bf16[1024,512]{1,0:T(8,128)(2,1)}, bf16[1024,512]{1,0:T(8,128)(2,1)S(1)}, u32[]{:S(2)}, u32[]{:S(2)}) collective-permute-start(bf16[1024,512]{1,0:T(8,128)(2,1)} %anom.3), channel_id=1, source_target_pairs={{0,1},{17,16},{2,3},{19,18},{4,5},{21,20},{6,7},{23,22},{8,9},{25,... | collective-permute-start | bytes 3145736 | tf_op jit(solution)/shard_map/ppermute | solution.py:343
  7.9 1.5 %shard_map.78 = (bf16[1024,512]{1,0:T(8,128)(2,1)S(1)}, bf16[1024,512]{1,0:T(8,128)(2,1)S(1)}, bf16[8,3,128,128]{3,2,1,0:T(8,128)(2,1)S(1)}) custom-call(f32[1,512]{1,0:T(1,128)} %innov.3, s32[1,512]{1,0:T(1,128)} %cell.3, bf16[1024,512]{1,0:T(8,128)(2,1)} %anom.3, bf16[8,3,128,128]{3,2,1,0:T(8,128)(2,1)} %loc.1), custom_call_target="tpu_custom_call" | custom-call | flops 1000000 | bytes 4000000 | tf_op jit(solution)/shard_map/pallas_call | solution.py:38
  9.4 0.0 collective-permute-done.before
  9.4 1.6 %collective-permute-done.1.after = bf16[128,512]{1,0:T(8,128)(2,1)S(1)} collective-permute-done((bf16[128,512]{1,0:T(8,128)(2,1)S(1)}, bf16[128,512]{1,0:T(8,128)(2,1)S(1)}, u32[]{:S(2)}, u32[]{:S(2)}) %collective-permute-start.1) | collective-permute-done | bytes 131104 | tf_op jit(solution)/shard_map/ppermute | solution.py:345
  11.0 0.7 shard_map.79.mine
  11.7 3.2 %collective-permute-start.2 = (bf16[1024,512]{1,0:T(8,128)(2,1)S(1)}, bf16[1024,512]{1,0:T(8,128)(2,1)S(1)}, u32[]{:S(2)}, u32[]{:S(2)}) collective-permute-start(bf16[1024,512]{1,0:T(8,128)(2,1)S(1)} %shard_map.79.mine), channel_id=1, source_target_pairs={{0,16},{16,0},{1,17},{17,1},{2,18},{18,2},{3,19},{19,3},{4,20},{20... | collective-permute-start | bytes 3145736 | tf_op jit(solution)/shard_map/ppermute | solution.py:378
  15.0 9.3 %collective-permute-done.3.fetched = bf16[1024,512]{1,0:T(8,128)(2,1)S(1)} collective-permute-done((bf16[1024,512]{1,0:T(8,128)(2,1)}, bf16[1024,512]{1,0:T(8,128)(2,1)S(1)}, u32[]{:S(2)}, u32[]{:S(2)}) %collective-permute-start.3) | collective-permute-done | bytes 1048608 | tf_op jit(solution)/shard_map/ppermute | solution.py:343
  24.3 0.0 collective-permute-done.2.theirs
  24.3 2.3 %shard_map.80 = bf16[512,1024]{1,0:T(8,128)(2,1)} custom-call(bf16[1024,512]{1,0:T(8,128)(2,1)S(1)} %shard_map.79.mine, bf16[1024,512]{1,0:T(8,128)(2,1)S(1)} %collective-permute-done.2.theirs, bf16[1024,512]{1,0:T(8,128)(2,1)S(1)} %get-tuple-element.25.anom, bf16[1024,512]{1,0:T(8,128)(2,1)S(1)} %collective-permute-done.3.fetched), custom_call_target="tpu_custom_call" | custom-call | flops 1000000000 | bytes 3000000 | tf_op jit(solution)/shard_map/pallas_call | solution.py:38
  26.6 4.6 %all-to-all-start = ((bf16[8,64,1024]{2,1,0:T(8,128)(2,1)}), bf16[8,64,1024]{2,1,0:T(8,128)(2,1)S(1)}, u32[]{:S(2)}, u32[]{:S(2)}) async-start(bf16[8,64,1024]{2,1,0:T(8,128)(2,1)} %bitcast.1), calls=%async_computation | async-start | bytes 2097152 | tf_op jit(solution)/shard_map/all_to_all | solution.py:383
  31.1 0.0 collective-permute-start.5
  31.1 1.5 %collective-permute-done.5.oth = bf16[1040,128]{1,0:T(8,128)(2,1)S(1)} collective-permute-done((bf16[1040,128]{1,0:T(8,128)(2,1)S(1)}, bf16[1040,128]{1,0:T(8,128)(2,1)S(1)}, u32[]{:S(2)}, u32[]{:S(2)}) %collective-permute-start.5) | collective-permute-done | bytes 266272 | tf_op jit(solution)/shard_map/ppermute | solution.py:346
  32.7 1.3 %shard_map.82 = (bf16[2,1024,128]{2,1,0:T(8,128)(2,1)S(1)}, bf16[1040,128]{1,0:T(8,128)(2,1)S(1)}, s32[8,128]{1,0:T(8,128)S(1)}) custom-call(bf16[1040,128]{1,0:T(8,128)(2,1)S(1)} %get-tuple-element.28.own, bf16[1040,128]{1,0:T(8,128)(2,1)S(1)} %collective-permute-done.5.oth), custom_call_target="tpu_custom_call" | custom-call | flops 10000000 | bytes 2000000 | tf_op jit(solution)/shard_map/pallas_call | solution.py:38
  34.0 5.7 %collective-permute-start.6 = (bf16[1040,128]{1,0:T(8,128)(2,1)S(1)}, bf16[1040,128]{1,0:T(8,128)(2,1)S(1)}, u32[]{:S(2)}, u32[]{:S(2)}) collective-permute-start(bf16[1040,128]{1,0:T(8,128)(2,1)S(1)} %get-tuple-element.31), channel_id=1, source_target_pairs={{0,32},{48,16},{32,64},{80,48},{64,96},{112,80},{96,128},{144,112}... | collective-permute-start | bytes 798728 | tf_op jit(solution)/shard_map/ppermute | solution.py:364
  39.6 3.4 %collective-permute-done.6.refs_0_ = bf16[1040,128]{1,0:T(8,128)(2,1)S(1)} collective-permute-done((bf16[1040,128]{1,0:T(8,128)(2,1)S(1)}, bf16[1040,128]{1,0:T(8,128)(2,1)S(1)}, u32[]{:S(2)}, u32[]{:S(2)}) %collective-permute-start.6) | collective-permute-done | bytes 266272 | tf_op jit(solution)/shard_map/ppermute | solution.py:364
  43.0 3.4 %collective-permute-start.7 = (bf16[1040,128]{1,0:T(8,128)(2,1)S(1)}, bf16[1040,128]{1,0:T(8,128)(2,1)S(1)}, u32[]{:S(2)}, u32[]{:S(2)}) collective-permute-start(bf16[1040,128]{1,0:T(8,128)(2,1)S(1)} %collective-permute-done.6.refs_0_), channel_id=1, source_target_pairs={{0,32},{48,16},{32,64},{80,48},{64,96},{112,80},{96,128},{144,112}... | collective-permute-start | bytes 798728 | tf_op jit(solution)/shard_map/ppermute | solution.py:364
  46.4 0.7 all-to-all-done.parts
  47.1 0.1 shard_map.81
  47.3 0.8 collective-permute-start.4
  48.0 0.9 collective-permute-done.4.oth
  48.9 1.9 %shard_map.83 = bf16[8,32,1024]{2,1,0:T(8,128)(2,1)} custom-call(f32[32,1024]{1,0:T(8,128)S(1)} %get-tuple-element.26.own, bf16[32,1024]{1,0:T(8,128)(2,1)S(1)} %collective-permute-done.4.oth, bf16[2,1024,128]{2,1,0:T(8,128)(2,1)S(1)} %get-tuple-element.29.both, s32[8,128]{1,0:T(8,128)S(1)} %get-tuple-element.30.ords), custom_call_target="tpu_custom_call" | custom-call | flops 100000000 | bytes 1000000 | tf_op jit(solution)/shard_map/pallas_call | solution.py:38
  50.9 8.2 %all-to-all-start.1 = ((bf16[8,32,1024]{2,1,0:T(8,128)(2,1)}), bf16[8,32,1024]{2,1,0:T(8,128)(2,1)S(1)}, u32[]{:S(2)}, u32[]{:S(2)}) async-start(bf16[8,32,1024]{2,1,0:T(8,128)(2,1)} %shard_map.83), calls=%async_computation.1 | async-start | bytes 1048576 | tf_op jit(solution)/shard_map/all_to_all | solution.py:398
  59.1 0.0 collective-permute-done.7.refs_1_
  59.1 2.7 %collective-permute-start.8 = (bf16[1040,128]{1,0:T(8,128)(2,1)S(1)}, bf16[1040,128]{1,0:T(8,128)(2,1)S(1)}, u32[]{:S(2)}, u32[]{:S(2)}) collective-permute-start(bf16[1040,128]{1,0:T(8,128)(2,1)S(1)} %collective-permute-done.7.refs_1_), channel_id=1, source_target_pairs={{0,32},{48,16},{32,64},{80,48},{64,96},{112,80},{96,128},{144,112}... | collective-permute-start | bytes 798728 | tf_op jit(solution)/shard_map/ppermute | solution.py:364
  61.7 14.3 %collective-permute-done.8.refs_2_ = bf16[1040,128]{1,0:T(8,128)(2,1)S(1)} collective-permute-done((bf16[1040,128]{1,0:T(8,128)(2,1)S(1)}, bf16[1040,128]{1,0:T(8,128)(2,1)S(1)}, u32[]{:S(2)}, u32[]{:S(2)}) %collective-permute-start.8) | collective-permute-done | bytes 266272 | tf_op jit(solution)/shard_map/ppermute | solution.py:364
  76.1 1.2 %collective-permute-start.9 = (bf16[1040,128]{1,0:T(8,128)(2,1)S(1)}, bf16[1040,128]{1,0:T(8,128)(2,1)S(1)}, u32[]{:S(2)}, u32[]{:S(2)}) collective-permute-start(bf16[1040,128]{1,0:T(8,128)(2,1)S(1)} %collective-permute-done.8.refs_2_), channel_id=1, source_target_pairs={{0,32},{48,16},{32,64},{80,48},{64,96},{112,80},{96,128},{144,112}... | collective-permute-start | bytes 798728 | tf_op jit(solution)/shard_map/ppermute | solution.py:364
  77.2 4.1 %collective-permute-done.9.refs_3_ = bf16[1040,128]{1,0:T(8,128)(2,1)S(1)} collective-permute-done((bf16[1040,128]{1,0:T(8,128)(2,1)S(1)}, bf16[1040,128]{1,0:T(8,128)(2,1)S(1)}, u32[]{:S(2)}, u32[]{:S(2)}) %collective-permute-start.9) | collective-permute-done | bytes 266272 | tf_op jit(solution)/shard_map/ppermute | solution.py:364
  81.3 3.7 %collective-permute-start.10 = (bf16[1040,128]{1,0:T(8,128)(2,1)S(1)}, bf16[1040,128]{1,0:T(8,128)(2,1)S(1)}, u32[]{:S(2)}, u32[]{:S(2)}) collective-permute-start(bf16[1040,128]{1,0:T(8,128)(2,1)S(1)} %collective-permute-done.6.refs_0_), channel_id=1, source_target_pairs={{0,16},{16,0},{1,17},{17,1},{2,18},{18,2},{3,19},{19,3},{4,20},{20... | collective-permute-start | bytes 798728 | tf_op jit(solution)/shard_map/ppermute | solution.py:403
  85.1 0.0 collective-permute-start.11
  85.1 0.5 collective-permute-start.12
  85.6 0.7 collective-permute-done.10.refs_4_
  86.2 0.4 collective-permute-done.11.refs_5_
  86.6 0.4 collective-permute-done.12.refs_6_
  87.0 1.4 %shard_map.84 = (bf16[8,1024,128]{2,1,0:T(8,128)(2,1)S(1)}, s32[8,128]{1,0:T(8,128)S(1)}) custom-call(bf16[1040,128]{1,0:T(8,128)(2,1)S(1)} %collective-permute-done.6.refs_0_, bf16[1040,128]{1,0:T(8,128)(2,1)S(1)} %collective-permute-done.7.refs_1_, bf16[1040,128]{1,0:T(8,128)(2,1)S(1)} %collective-permute-done.8.refs_2_, ...), custom_call_target="tpu_custom_call" | custom-call | flops 1000000 | bytes 4000000 | tf_op jit(solution)/shard_map/pallas_call | solution.py:38
  88.4 0.0 copy-start
  88.4 1.3 %copy-done = bf16[8,1024,128]{2,1,0:T(8,128)(2,1)} copy-done((bf16[8,1024,128]{2,1,0:T(8,128)(2,1)}, bf16[8,1024,128]{2,1,0:T(8,128)(2,1)S(1)}, u32[]{:S(2)}) %copy-start) | copy-done | bytes 2097176
  89.7 0.0 all-to-all-done.1.recv
  89.7 3.8 %shard_map.85 = (f32[2,32,1024]{2,1,0:T(8,128)S(1)}, bf16[2,32,1024]{2,1,0:T(8,128)(2,1)S(1)}) custom-call(bf16[8,32,1024]{2,1,0:T(8,128)(2,1)S(1)} %all-to-all-done.1.recv, bf16[8,1024,128]{2,1,0:T(8,128)(2,1)} %copy-done, s32[8,128]{1,0:T(8,128)S(1)} %get-tuple-element.37.tags, bf16[2,1024,128]{2,1,0:T(8,128)(2,1)S(1)} %get-tuple-element.29.both, ...), custom_call_target="tpu_custom_call" | custom-call | flops 1000000000 | bytes 3000000 | tf_op jit(solution)/shard_map/pallas_call | solution.py:38
  93.5 0.5 collective-permute-start.13
  94.0 1.0 %collective-permute-done.13.back = bf16[2,32,1024]{2,1,0:T(8,128)(2,1)S(1)} collective-permute-done((bf16[2,32,1024]{2,1,0:T(8,128)(2,1)S(1)}, bf16[2,32,1024]{2,1,0:T(8,128)(2,1)S(1)}, u32[]{:S(2)}, u32[]{:S(2)}) %collective-permute-start.13) | collective-permute-done | bytes 131104 | tf_op jit(solution)/shard_map/ppermute | solution.py:428
  94.9 0.8 shard_map.86
Async XLA Ops:
  1.9 7.5 %collective-permute-start = (bf16[128,512]{1,0:T(8,128)(2,1)S(1)}, bf16[128,512]{1,0:T(8,128)(2,1)S(1)}, u32[]{:S(2)}, u32[]{:S(2)}) collective-permute-start(bf16[128,512]{1,0:T(8,128)(2,1)S(1)} %get-tuple-element.21), channel_id=1, source_target_pairs={{0,2},{2,4},{4,6},{6,8},{8,10},{10,12},{12,14},{14,0},{1,3},{3,5},... | collective-permute-start | bytes 393224 | tf_op jit(solution)/shard_map/ppermute | solution.py:344
  4.0 7.0 %collective-permute-start.1 = (bf16[128,512]{1,0:T(8,128)(2,1)S(1)}, bf16[128,512]{1,0:T(8,128)(2,1)S(1)}, u32[]{:S(2)}, u32[]{:S(2)}) collective-permute-start(bf16[128,512]{1,0:T(8,128)(2,1)S(1)} %get-tuple-element.23), channel_id=1, source_target_pairs={{2,0},{4,2},{6,4},{8,6},{10,8},{12,10},{14,12},{0,14},{3,1},{5,3},... | collective-permute-start | bytes 393224 | tf_op jit(solution)/shard_map/ppermute | solution.py:345
  6.6 17.7 %collective-permute-start.3 = (bf16[1024,512]{1,0:T(8,128)(2,1)}, bf16[1024,512]{1,0:T(8,128)(2,1)S(1)}, u32[]{:S(2)}, u32[]{:S(2)}) collective-permute-start(bf16[1024,512]{1,0:T(8,128)(2,1)} %anom.3), channel_id=1, source_target_pairs={{0,1},{17,16},{2,3},{19,18},{4,5},{21,20},{6,7},{23,22},{8,9},{25,... | collective-permute-start | bytes 3145736 | tf_op jit(solution)/shard_map/ppermute | solution.py:343
  11.7 12.5 %collective-permute-start.2 = (bf16[1024,512]{1,0:T(8,128)(2,1)S(1)}, bf16[1024,512]{1,0:T(8,128)(2,1)S(1)}, u32[]{:S(2)}, u32[]{:S(2)}) collective-permute-start(bf16[1024,512]{1,0:T(8,128)(2,1)S(1)} %shard_map.79.mine), channel_id=1, source_target_pairs={{0,16},{16,0},{1,17},{17,1},{2,18},{18,2},{3,19},{19,3},{4,20},{20... | collective-permute-start | bytes 3145736 | tf_op jit(solution)/shard_map/ppermute | solution.py:378
  26.6 20.6 %all-to-all-start = ((bf16[8,64,1024]{2,1,0:T(8,128)(2,1)}), bf16[8,64,1024]{2,1,0:T(8,128)(2,1)S(1)}, u32[]{:S(2)}, u32[]{:S(2)}) async-start(bf16[8,64,1024]{2,1,0:T(8,128)(2,1)} %bitcast.1), calls=%async_computation | async-start | bytes 2097152 | tf_op jit(solution)/shard_map/all_to_all | solution.py:383
  31.1 1.5 %collective-permute-start.5 = (bf16[1040,128]{1,0:T(8,128)(2,1)S(1)}, bf16[1040,128]{1,0:T(8,128)(2,1)S(1)}, u32[]{:S(2)}, u32[]{:S(2)}) collective-permute-start(bf16[1040,128]{1,0:T(8,128)(2,1)S(1)} %get-tuple-element.28.own), channel_id=1, source_target_pairs={{0,16},{16,0},{1,17},{17,1},{2,18},{18,2},{3,19},{19,3},{4,20},{20... | collective-permute-start | bytes 798728 | tf_op jit(solution)/shard_map/ppermute | solution.py:346
  34.0 9.0 %collective-permute-start.6 = (bf16[1040,128]{1,0:T(8,128)(2,1)S(1)}, bf16[1040,128]{1,0:T(8,128)(2,1)S(1)}, u32[]{:S(2)}, u32[]{:S(2)}) collective-permute-start(bf16[1040,128]{1,0:T(8,128)(2,1)S(1)} %get-tuple-element.31), channel_id=1, source_target_pairs={{0,32},{48,16},{32,64},{80,48},{64,96},{112,80},{96,128},{144,112}... | collective-permute-start | bytes 798728 | tf_op jit(solution)/shard_map/ppermute | solution.py:364
  43.0 16.1 %collective-permute-start.7 = (bf16[1040,128]{1,0:T(8,128)(2,1)S(1)}, bf16[1040,128]{1,0:T(8,128)(2,1)S(1)}, u32[]{:S(2)}, u32[]{:S(2)}) collective-permute-start(bf16[1040,128]{1,0:T(8,128)(2,1)S(1)} %collective-permute-done.6.refs_0_), channel_id=1, source_target_pairs={{0,32},{48,16},{32,64},{80,48},{64,96},{112,80},{96,128},{144,112}... | collective-permute-start | bytes 798728 | tf_op jit(solution)/shard_map/ppermute | solution.py:364
  47.3 1.7 %collective-permute-start.4 = (bf16[32,1024]{1,0:T(8,128)(2,1)S(1)}, bf16[32,1024]{1,0:T(8,128)(2,1)S(1)}, u32[]{:S(2)}, u32[]{:S(2)}) collective-permute-start(bf16[32,1024]{1,0:T(8,128)(2,1)S(1)} %get-tuple-element.27), channel_id=1, source_target_pairs={{0,16},{16,0},{1,17},{17,1},{2,18},{18,2},{3,19},{19,3},{4,20},{20... | collective-permute-start | bytes 196616 | tf_op jit(solution)/shard_map/ppermute | solution.py:389
  50.9 38.8 %all-to-all-start.1 = ((bf16[8,32,1024]{2,1,0:T(8,128)(2,1)}), bf16[8,32,1024]{2,1,0:T(8,128)(2,1)S(1)}, u32[]{:S(2)}, u32[]{:S(2)}) async-start(bf16[8,32,1024]{2,1,0:T(8,128)(2,1)} %shard_map.83), calls=%async_computation.1 | async-start | bytes 1048576 | tf_op jit(solution)/shard_map/all_to_all | solution.py:398
  59.1 17.0 %collective-permute-start.8 = (bf16[1040,128]{1,0:T(8,128)(2,1)S(1)}, bf16[1040,128]{1,0:T(8,128)(2,1)S(1)}, u32[]{:S(2)}, u32[]{:S(2)}) collective-permute-start(bf16[1040,128]{1,0:T(8,128)(2,1)S(1)} %collective-permute-done.7.refs_1_), channel_id=1, source_target_pairs={{0,32},{48,16},{32,64},{80,48},{64,96},{112,80},{96,128},{144,112}... | collective-permute-start | bytes 798728 | tf_op jit(solution)/shard_map/ppermute | solution.py:364
  76.1 5.3 %collective-permute-start.9 = (bf16[1040,128]{1,0:T(8,128)(2,1)S(1)}, bf16[1040,128]{1,0:T(8,128)(2,1)S(1)}, u32[]{:S(2)}, u32[]{:S(2)}) collective-permute-start(bf16[1040,128]{1,0:T(8,128)(2,1)S(1)} %collective-permute-done.8.refs_2_), channel_id=1, source_target_pairs={{0,32},{48,16},{32,64},{80,48},{64,96},{112,80},{96,128},{144,112}... | collective-permute-start | bytes 798728 | tf_op jit(solution)/shard_map/ppermute | solution.py:364
  81.3 4.9 %collective-permute-start.10 = (bf16[1040,128]{1,0:T(8,128)(2,1)S(1)}, bf16[1040,128]{1,0:T(8,128)(2,1)S(1)}, u32[]{:S(2)}, u32[]{:S(2)}) collective-permute-start(bf16[1040,128]{1,0:T(8,128)(2,1)S(1)} %collective-permute-done.6.refs_0_), channel_id=1, source_target_pairs={{0,16},{16,0},{1,17},{17,1},{2,18},{18,2},{3,19},{19,3},{4,20},{20... | collective-permute-start | bytes 798728 | tf_op jit(solution)/shard_map/ppermute | solution.py:403
  85.1 1.5 %collective-permute-start.11 = (bf16[1040,128]{1,0:T(8,128)(2,1)S(1)}, bf16[1040,128]{1,0:T(8,128)(2,1)S(1)}, u32[]{:S(2)}, u32[]{:S(2)}) collective-permute-start(bf16[1040,128]{1,0:T(8,128)(2,1)S(1)} %collective-permute-done.7.refs_1_), channel_id=1, source_target_pairs={{0,16},{16,0},{1,17},{17,1},{2,18},{18,2},{3,19},{19,3},{4,20},{20... | collective-permute-start | bytes 798728 | tf_op jit(solution)/shard_map/ppermute | solution.py:403
  85.1 1.9 %collective-permute-start.12 = (bf16[1040,128]{1,0:T(8,128)(2,1)S(1)}, bf16[1040,128]{1,0:T(8,128)(2,1)S(1)}, u32[]{:S(2)}, u32[]{:S(2)}) collective-permute-start(bf16[1040,128]{1,0:T(8,128)(2,1)S(1)} %collective-permute-done.8.refs_2_), channel_id=1, source_target_pairs={{0,16},{16,0},{1,17},{17,1},{2,18},{18,2},{3,19},{19,3},{4,20},{20... | collective-permute-start | bytes 798728 | tf_op jit(solution)/shard_map/ppermute | solution.py:403
  88.4 1.3 %copy-start = (bf16[8,1024,128]{2,1,0:T(8,128)(2,1)}, bf16[8,1024,128]{2,1,0:T(8,128)(2,1)S(1)}, u32[]{:S(2)}) copy-start(bf16[8,1024,128]{2,1,0:T(8,128)(2,1)S(1)} %get-tuple-element.36.stored) | copy-start | bytes 6291460
  93.5 1.4 %collective-permute-start.13 = (bf16[2,32,1024]{2,1,0:T(8,128)(2,1)S(1)}, bf16[2,32,1024]{2,1,0:T(8,128)(2,1)S(1)}, u32[]{:S(2)}, u32[]{:S(2)}) collective-permute-start(bf16[2,32,1024]{2,1,0:T(8,128)(2,1)S(1)} %get-tuple-element.39), channel_id=1, source_target_pairs={{0,16},{16,0},{1,17},{17,1},{2,18},{18,2},{3,19},{19,3},{4,20},{20... | collective-permute-start | bytes 393224 | tf_op jit(solution)/shard_map/ppermute | solution.py:428
